TPU v7x, 512 devices: a whole 4x8x8 slice. The times are simulated.
512 devices in a mesh: nest: 8 (over x, z_hi), gx: 8 (over y), gy: 8 (over z_lo, core).
Axes of the slice: x: 4, y: 8, z: 8 (z_hi: 2, z_lo: 4; z = z_hi * 4 + z_lo), core: 2. Of those that a mesh axis runs over, the one named last changes fastest.
Arguments:
- state: float32 [8, 4, 8, 128, 1024], P('nest', None, None, 'gx', 'gy'), may hold values from -6 to 6
- metric: float32 [8, 3, 128, 1024], P('nest', None, 'gx', 'gy'), may hold values from -1.2 to 1.4, as said below
- placement: int32 [7, 2], replicated, may hold values from 0 to 682, as said below
- zones: int32 [7, 4], replicated, may hold values from 2 to 5
Outputs:
- new_state: float32 [8, 4, 8, 128, 1024], P('nest', None, None, 'gx', 'gy')
Inputs may be any that keep to these rules, and one draw needn't show every extreme that they name: metric[:, 0] and metric[:, 1] are terrain slopes; metric[:, 2] is the column stretch, between 0.6 and 1.4. placement[n] = (ox, oy) with ox <= 85 and oy <= 682.
All inputs are finite; a program needn't handle non-finite values.
Results may differ from a plain program's by a relative error of at most 0.0003.
Values sent between devices are 32-bit elements; how exact they have to be, the bound alone decides.
No kernel may reach another device: no remote copies, remote signals or barrier semaphores. Data moves between devices by JAX's collectives and lax.ppermute only.
A program may use at most 64 MiB of HBM per device.

v0:
```python
import jax
import jax.numpy as jnp
from jax import lax
from jax.sharding import PartitionSpec as P

SUB = 4
R = 3
W_MAX = 5
WP = 3


TIME_STEP = 0.5
SOUND_SQ = 1.0
PRECISE = lax.Precision.HIGHEST


def extended(value, sides, width):
    for axis, dim in sides:
        devices, length = (lax.axis_size(axis), value.shape[dim])
        up = [(i, (i + 1) % devices) for i in range(devices - 1)]
        down = [(j, i) for i, j in up]
        last = lax.slice_in_dim(value, length - width, length, axis=dim)
        initial = lax.slice_in_dim(value, 0, width, axis=dim)
        before = lax.ppermute(last, axis, up)
        after = lax.ppermute(initial, axis, down)
        value = jnp.concatenate([before, value, after], axis=dim)
    return value


def broadcast(block, axis, owner):
    block = jnp.where(lax.axis_index(axis) == owner, block, jnp.zeros_like(block))
    return lax.psum(block, axis)


def vertical(field):
    upper = jnp.concatenate([field[1:], field[-1:]], 0)
    lower = jnp.concatenate([field[:1], field[:-1]], 0)
    return (upper - lower) * 0.5


def edge_weight(zone_width, row_index, col_index, total_x, total_y):
    widths = zone_width.astype(jnp.float32)
    row_pos = row_index.astype(jnp.float32)[:, None]
    col_pos = col_index.astype(jnp.float32)[None, :]
    dists = (row_pos, total_x - 1 - row_pos, col_pos, total_y - 1 - col_pos)
    weight = jnp.zeros((row_index.shape[0], col_index.shape[0]), jnp.float32)
    for edge in range(4):
        weight = jnp.maximum(weight, jnp.maximum((widths[edge] - dists[edge]) / widths[edge], 0.0))
    return weight


def step_each(current, terrain, sigma_col):
    wind_x, wind_y, updraft, pressure = current
    pressure_ext = extended(pressure, (("gx", 1), ("gy", 2)), 1)
    press_z = vertical(pressure) / terrain[2]
    grad_x = (pressure_ext[:, 2:, 1:-1] - pressure_ext[:, :-2, 1:-1]) * 0.5
    grad_y = (pressure_ext[:, 1:-1, 2:] - pressure_ext[:, 1:-1, :-2]) * 0.5
    new_x = wind_x - TIME_STEP * (grad_x - sigma_col * terrain[0] * press_z)
    new_y = wind_y - TIME_STEP * (grad_y - sigma_col * terrain[1] * press_z)
    new_w = updraft - TIME_STEP * press_z
    winds_ext = extended(jnp.stack([new_x, new_y]), (("gx", 2), ("gy", 3)), 1)
    spread = (winds_ext[0, :, 2:, 1:-1] - winds_ext[0, :, :-2, 1:-1]) * 0.5 + (
        winds_ext[1, :, 1:-1, 2:] - winds_ext[1, :, 1:-1, :-2]
    ) * 0.5
    spread = (
        spread
        - sigma_col * (terrain[0] * vertical(new_x) + terrain[1] * vertical(new_y)) / terrain[2]
        + vertical(new_w) / terrain[2]
    )
    return (new_x, new_y, new_w, pressure - TIME_STEP * SOUND_SQ * spread)


def boundary_pieces(
    parent_tile, placement, row_start, col_start, total_x, total_y, foot_x, foot_y, span_len
):
    row_index = row_start + jnp.arange(parent_tile.shape[2], dtype=jnp.int32)
    col_index = col_start + jnp.arange(parent_tile.shape[3], dtype=jnp.int32)
    depth_range = jnp.arange(WP, dtype=jnp.int32)
    reach_range = jnp.arange(span_len, dtype=jnp.int32)
    west_x = placement[:, 0:1]
    south_y = placement[:, 1:2]
    east_base = (total_x - 1) // R - (WP - 1)
    north_base = (total_y - 1) // R - (WP - 1)
    x_depth = jnp.stack([west_x + depth_range, west_x + east_base + depth_range], 1)
    y_depth = jnp.stack([south_y + depth_range, south_y + north_base + depth_range], 1)
    x_reach = jnp.where(reach_range < foot_x, west_x + reach_range, -1)
    y_reach = jnp.where(reach_range < foot_y, south_y + reach_range, -1)
    pick_rows = (x_depth[..., None] == row_index).astype(jnp.float32)
    pick_cols = (y_reach[:, None, :] == col_index[None, :, None]).astype(jnp.float32)
    across = jnp.einsum("neai,flij->neflaj", pick_rows, parent_tile, precision=PRECISE)
    across = jnp.einsum("neflaj,njb->neflab", across, pick_cols, precision=PRECISE)
    pick_depth = (y_depth[..., None] == col_index).astype(jnp.float32)
    pick_reach = (x_reach[:, None, :] == row_index[None, :, None]).astype(jnp.float32)
    along_y = jnp.einsum("neaj,flij->neflai", pick_depth, parent_tile, precision=PRECISE)
    along_y = jnp.einsum("neflai,nib->neflab", along_y, pick_reach, precision=PRECISE)
    return jnp.concatenate([across, along_y], 1)


def relax_edges(relaxed_in, own_pieces, zone_width, row_start, col_start, total_x, total_y, active):
    row_index = row_start + jnp.arange(relaxed_in.shape[2], dtype=jnp.int32)
    col_index = col_start + jnp.arange(relaxed_in.shape[3], dtype=jnp.int32)
    depth_range = jnp.arange(WP, dtype=jnp.int32)
    reach_range = jnp.arange(own_pieces.shape[-1], dtype=jnp.int32)
    east_base = (total_x - 1) // R - (WP - 1)
    north_base = (total_y - 1) // R - (WP - 1)
    west_pick = ((row_index < W_MAX)[:, None] & ((row_index // R)[:, None] == depth_range)).astype(
        jnp.float32
    )
    east_pick = (
        (row_index >= total_x - W_MAX)[:, None]
        & ((row_index // R - east_base)[:, None] == depth_range)
    ).astype(jnp.float32)
    south_pick = ((col_index < W_MAX)[:, None] & ((col_index // R)[:, None] == depth_range)).astype(
        jnp.float32
    )
    north_pick = (
        (col_index >= total_y - W_MAX)[:, None]
        & ((col_index // R - north_base)[:, None] == depth_range)
    ).astype(jnp.float32)
    col_reach = (reach_range[:, None] == (col_index // R)[None, :]).astype(jnp.float32)
    row_reach = (reach_range[:, None] == (row_index // R)[None, :]).astype(jnp.float32)
    across = jnp.einsum("eflab,bj->eflaj", own_pieces[0:2], col_reach, precision=PRECISE)
    from_x = jnp.einsum("ia,flaj->flij", west_pick, across[0], precision=PRECISE) + jnp.einsum(
        "ia,flaj->flij", east_pick, across[1], precision=PRECISE
    )
    along_y = jnp.einsum("eflab,bi->eflai", own_pieces[2:4], row_reach, precision=PRECISE)
    from_y = jnp.einsum("ja,flai->flij", south_pick, along_y[0], precision=PRECISE) + jnp.einsum(
        "ja,flai->flij", north_pick, along_y[1], precision=PRECISE
    )
    in_x = (row_index < W_MAX) | (row_index >= total_x - W_MAX)
    target = jnp.where(in_x[:, None], from_x, from_y)
    weight = edge_weight(zone_width, row_index, col_index, total_x, total_y)
    weight = jnp.where(active, weight, 0.0)
    return relaxed_in + weight * (target - relaxed_in)


def local(state, metric, placement, zones):
    fields = state[0]
    terrain = metric[0]
    levels, size_x, size_y = (fields.shape[1], fields.shape[2], fields.shape[3])
    total_x = size_x * lax.axis_size("gx")
    total_y = size_y * lax.axis_size("gy")
    nest_count = placement.shape[0]
    group_index = lax.axis_index("nest")
    row_start = lax.axis_index("gx") * size_x
    col_start = lax.axis_index("gy") * size_y
    foot_x = (total_x + R - 1) // R
    foot_y = (total_y + R - 1) // R
    span_len = 64 * ((max(foot_x, foot_y) + 63) // 64)
    own_group = jnp.minimum(group_index, nest_count - 1)
    start_three = jnp.stack([fields[0], fields[1], fields[3]])
    pieces = boundary_pieces(
        start_three, placement, row_start, col_start, total_x, total_y, foot_x, foot_y, span_len
    )
    summed = lax.psum(pieces, ("gx", "gy"))
    arrived = broadcast(summed, "nest", nest_count)
    own_pieces = arrived[own_group]
    sigma_col = (1.0 - (jnp.arange(levels, dtype=jnp.float32) + 0.5) / levels)[:, None, None]
    current = (fields[0], fields[1], fields[2], fields[3])
    for substep in range(SUB):
        current = step_each(current, terrain, sigma_col)
    active = group_index < nest_count
    moved_three = jnp.stack([current[0], current[1], current[3]])
    relaxed = relax_edges(
        moved_three, own_pieces, zones[own_group], row_start, col_start, total_x, total_y, active
    )
    result = jnp.stack([relaxed[0], relaxed[1], current[2], relaxed[2]])
    return result[None]


def solution(mesh):
    return jax.shard_map(
        local,
        mesh=mesh,
        in_specs=(P("nest", None, None, "gx", "gy"), P("nest", None, "gx", "gy"), P(), P()),
        out_specs=P("nest", None, None, "gx", "gy"),
        check_vma=False,
    )
```

profile of v0, /device:TPU:1, one launch (start us, length us, event | category | flops | bytes accessed | tf_op | source)
XLA Modules:
  0.0 865.6 jit_solution(14164995903394578647)
XLA Ops:
  11.9 1.9 pad_maximum_fusion
  13.9 4.2 collective-permute-start.1
  23.2 5.4 collective-permute-start.3
  28.5 2.5 collective-permute-start.2
  31.2 3.3 collective-permute-done.2
  36.0 4.4 collective-permute-start.5
  41.3 2.7 collective-permute-start.7
  46.7 5.1 collective-permute-done.6
  52.0 3.6 collective-permute-start.9
  57.0 5.0 collective-permute-done.8
  62.1 2.5 collective-permute-start.11
  66.7 3.9 collective-permute-done.10
  72.1 5.1 collective-permute-start.13
  78.1 2.7 collective-permute-start.15
  83.4 4.7 collective-permute-done.14
  88.3 6.4 collective-permute-start.17
  96.0 3.9 collective-permute-done.16
  100.1 2.1 collective-permute-start.19
  102.2 2.2 collective-permute-start.18
  104.5 4.1 collective-permute-done.18
  110.1 4.9 collective-permute-start.21
  115.9 2.7 collective-permute-start.23
  121.5 6.1 collective-permute-done.22
  127.8 4.3 collective-permute-start.25
  133.5 438.1 %all-reduce.3.cloned.1.call-done = f32[7,4,3,8,3,384]{5,3,4,2,1,0:T(8,128)} async-done(((f32[7,4,3,8,3,384]{5,3,4,2,1,0:T(8,128)}), f32[7,4,3,8,3,384]{5,3,4,2,1,0:T(8,128)}) %all-reduce.3.cloned.1.call-update) | async-done | bytes 3096592 | tf_op jit(solution)/shard_map/psum | solution.py:155
  575.6 3.8 collective-permute-start.26
  579.4 2.1 collective-permute-done.26
  583.0 4.0 collective-permute-start.29
  588.0 3.0 collective-permute-start.31
  592.9 5.6 collective-permute-done.31
  598.5 62.3 %collective-permute-done.30 = f32[2,8,18,1]{3,2,1,0:T(8,128)S(1)} collective-permute-done((f32[2,8,18,1]{3,2,1,0:T(8,128)S(1)}, f32[2,8,18,1]{3,2,1,0:T(8,128)S(1)}, u32[]{:S(2)}, u32[]{:S(2)}) %collective-permute-start.30) | collective-permute-done | bytes 1184 | tf_op jit(solution)/shard_map/ppermute | solution.py:25
  661.1 193.1 %all-reduce.5.cloned.1.call-done = f32[7,4,3,8,3,384]{5,3,4,2,1,0:T(8,128)} async-done(((f32[7,4,3,8,3,384]{5,3,4,2,1,0:T(8,128)}), f32[7,4,3,8,3,384]{5,3,4,2,1,0:T(8,128)}) %all-reduce.5.cloned.1.call-update) | async-done | bytes 3096592 | tf_op jit(solution)/shard_map/psum | solution.py:32
  (159 shorter events, 45.6 us)
Async XLA Ops:
  6.5 565.0 %all-reduce.3.cloned.1.call-start = ((), (), s32[]{:S(2)}) async-start(), calls=%async_computation | async-start | bytes 6193152 | tf_op jit(solution)/shard_map/psum | solution.py:155
  13.8 840.3 %all-reduce.5.cloned.1.call-start = ((), (), s32[]{:S(2)}) async-start(), calls=%async_computation.1 | async-start | bytes 6193152 | tf_op jit(solution)/shard_map/psum | solution.py:32
  13.9 9.1 %collective-permute-start.1 = (f32[8,1,128]{2,1,0:T(1,128)S(1)}, f32[8,1,128]{2,1,0:T(1,128)S(1)}, u32[]{:S(2)}, u32[]{:S(2)}) collective-permute-start(f32[8,1,128]{2,1,0:T(1,128)S(1)} %get-tuple-element.182), channel_id=1, source_target_pairs={{0,8},{8,16},{16,24},{24,32},{32,40},{40,48},{48,56},{1,9},{9,17},... | collective-permute-start | bytes 12296 | tf_op jit(solution)/shard_map/ppermute | solution.py:24
  18.1 5.0 collective-permute-start
  23.2 8.0 collective-permute-start.3
  28.5 5.9 collective-permute-start.2
  34.7 5.7 collective-permute-start.4
  36.0 5.2 collective-permute-start.5
  41.3 5.5 collective-permute-start.7
  44.0 7.8 collective-permute-start.6
  52.0 5.0 collective-permute-start.9
  55.7 6.3 collective-permute-start.8
  64.6 5.9 collective-permute-start.10
  70.8 6.4 collective-permute-start.12
  72.1 5.8 collective-permute-start.13
  78.1 5.3 collective-permute-start.15
  80.8 7.3 collective-permute-start.14
  88.3 7.7 collective-permute-start.17
  94.7 5.2 collective-permute-start.16
  102.2 6.4 collective-permute-start.18
  108.8 6.3 collective-permute-start.20
  110.1 5.7 collective-permute-start.21
  115.9 5.5 collective-permute-start.23
  118.6 9.0 %collective-permute-start.22 = (f32[2,8,18,1]{3,2,1,0:T(8,128)S(1)}, f32[2,8,18,1]{3,2,1,0:T(8,128)S(1)}, u32[]{:S(2)}, u32[]{:S(2)}) collective-permute-start(f32[2,8,18,1]{3,2,1,0:T(8,128)S(1)} %get-tuple-element.35), channel_id=1, source_target_pairs={{1,0},{2,1},{3,2},{4,3},{5,4},{6,5},{7,6},{9,8},{10,9},{11,10},{12... | collective-permute-start | bytes 3464 | tf_op jit(solution)/shard_map/ppermute | solution.py:25
  127.8 445.8 %collective-permute-start.25 = (f32[8,1,128]{2,1,0:T(1,128)S(1)}, f32[8,1,128]{2,1,0:T(1,128)S(1)}, u32[]{:S(2)}, u32[]{:S(2)}) collective-permute-start(f32[8,1,128]{2,1,0:T(1,128)S(1)} %get-tuple-element.171), channel_id=1, source_target_pairs={{0,8},{8,16},{16,24},{24,32},{32,40},{40,48},{48,56},{1,9},{9,17},... | collective-permute-start | bytes 12296 | tf_op jit(solution)/shard_map/ppermute | solution.py:24
  132.1 441.5 %collective-permute-start.24 = (f32[8,1,128]{2,1,0:T(1,128)S(1)}, f32[8,1,128]{2,1,0:T(1,128)S(1)}, u32[]{:S(2)}, u32[]{:S(2)}) collective-permute-start(f32[8,1,128]{2,1,0:T(1,128)S(1)} %get-tuple-element.172), channel_id=1, source_target_pairs={{8,0},{16,8},{24,16},{32,24},{40,32},{48,40},{56,48},{9,1},{17,9},... | collective-permute-start | bytes 12296 | tf_op jit(solution)/shard_map/ppermute | solution.py:25
  573.7 5.7 collective-permute-start.27
  575.6 5.9 collective-permute-start.26
  581.7 5.3 collective-permute-start.28
  583.0 4.8 collective-permute-start.29
  588.0 10.5 %collective-permute-start.31 = (f32[2,8,18,1]{3,2,1,0:T(8,128)S(1)}, f32[2,8,18,1]{3,2,1,0:T(8,128)S(1)}, u32[]{:S(2)}, u32[]{:S(2)}) collective-permute-start(f32[2,8,18,1]{3,2,1,0:T(8,128)S(1)} %get-tuple-element.34), channel_id=1, source_target_pairs={{0,1},{1,2},{2,3},{3,4},{4,5},{5,6},{6,7},{8,9},{9,10},{10,11},{11... | collective-permute-start | bytes 3464 | tf_op jit(solution)/shard_map/ppermute | solution.py:24
  590.9 69.9 %collective-permute-start.30 = (f32[2,8,18,1]{3,2,1,0:T(8,128)S(1)}, f32[2,8,18,1]{3,2,1,0:T(8,128)S(1)}, u32[]{:S(2)}, u32[]{:S(2)}) collective-permute-start(f32[2,8,18,1]{3,2,1,0:T(8,128)S(1)} %get-tuple-element.33), channel_id=1, source_target_pairs={{1,0},{2,1},{3,2},{4,3},{5,4},{6,5},{7,6},{9,8},{10,9},{11,10},{12... | collective-permute-start | bytes 3464 | tf_op jit(solution)/shard_map/ppermute | solution.py:25
  (5 other events, 26.2 us)
Sparse Core Ops, SparseCore 0:
  14.0 557.5 all-reduce.2
  574.5 279.5 all-reduce.4
where the time goes:
time: 867 us; the launch traced here: 866 us
  waiting for transfers between devices  743 us (86%)
  starting transfers between devices  88.2 us (10%)
  between operations  14.5 us (2%)
  other arithmetic  10.4 us (1%)
    psum x1, waiting for transfers between devices, local(): summed = lax.psum(pieces, ('gx', 'gy'))  438 us
    psum x1, waiting for transfers between devices, broadcast(): return lax.psum(block, axis)  193 us
    ppermute x16, waiting for transfers between devices, extended(): after = lax.ppermute(initial, axis, down)  100 us
    ppermute x16, starting transfers between devices, extended(): before = lax.ppermute(last, axis, up)  59.8 us
    ppermute x16, starting transfers between devices, extended(): after = lax.ppermute(initial, axis, down)  28.4 us
  transfers between devices with their start and end apart: 34, of which 20 were waited for; matrix products, arithmetic and copies ran while one was open for 1% of the time, Pallas kernels for 0%

commit v1 on v0

v1 whole, which is shorter than its diff:
```python
import jax
import jax.numpy as jnp
from jax import lax
from jax.experimental import pallas as pl
from jax.experimental.pallas import tpu as pltpu
from jax.sharding import PartitionSpec as P

SUB = 4
R = 3
W_MAX = 5
L = 8
NESTS = 7
HALO = 8
ROWS = 16
LANES = 128
PLANES = 4 * L + 3
SLOT = 64
X_ROWS = 48
N_X = 128
N_Y = 1024
EAST = (N_X - 1) // R - 1
NORTH = (N_Y - 1) // R - 2
F32 = jnp.float32
HIGH = lax.Precision.HIGHEST

VMEM_SPEC = pl.BlockSpec(memory_space=pltpu.VMEM)
SMEM_SPEC = pl.BlockSpec(memory_space=pltpu.SMEM)


def iota(shape, dim):
    return lax.broadcasted_iota(jnp.int32, shape, dim)


def plane_row(state, metric, plane, row, count):
    if plane < 4 * L:
        return state[plane * ROWS + row : plane * ROWS + row + count, :]
    start = (plane - 4 * L) * ROWS + row
    return metric[start : start + count, :]


def pack_kernel(state, metric, placement, slots, left, right):
    gx = lax.axis_index("gx")
    gy = lax.axis_index("gy")
    rows_n = iota((24, LANES), 0)
    first = jnp.zeros((24, LANES), jnp.int32)
    for n in range(NESTS):
        low = placement[n, 0] - ROWS * gx
        base = jnp.where((low >= -1) & (low < ROWS), low, low + EAST)
        for a in range(2):
            row = jnp.clip(base + a, 0, ROWS - 1)
            out = n * SLOT + a * 24
            slots[out : out + 16, :] = state[pl.ds(row, 16, stride=ROWS), :]
            slots[out + 16 : out + 24, :] = state[pl.ds(24 * ROWS + row, 8, stride=ROWS), :]
        low = placement[n, 1] - LANES * gy
        base = jnp.where((low >= -1) & (low < LANES), low, low + NORTH)
        first = jnp.where((rows_n >= 3 * n) & (rows_n < 3 * n + 3), base + rows_n - 3 * n, first)
    pick = (iota((24, LANES), 1) == first).astype(F32)
    for t in range(3):
        start = (0, 128, 384)[t]
        cols = lax.dot_general(
            pick, state[start : start + 128, :], (((1,), (1,)), ((), ())), precision=HIGH, preferred_element_type=F32
        )
        for n in range(NESTS):
            slots[n * SLOT + X_ROWS + 3 * t : n * SLOT + X_ROWS + 3 * t + 3, :] = cols[3 * n : 3 * n + 3, :]
    lane = iota((8, LANES), 1) // 8
    for rt in range(2):
        for group in range(3):
            left_sum = jnp.zeros((8, LANES), F32)
            right_sum = jnp.zeros((8, LANES), F32)
            for s in range(16):
                plane = group * 16 + s
                if plane >= PLANES:
                    break
                value = plane_row(state, metric, plane, rt * 8, 8)
                left_sum = jnp.where(lane == s, pltpu.roll(value, 8 * s, 1) if s else value, left_sum)
                shift = (8 * s + 8) % LANES
                right_sum = jnp.where(lane == s, pltpu.roll(value, shift, 1) if shift else value, right_sum)
            at = (rt * 3 + group) * 8
            left[at : at + 8, :] = left_sum
            right[at : at + 8, :] = right_sum


def join_kernel(state, metric, from_left, from_right, up, down):
    for plane in range(PLANES):
        up[plane * 8 : plane * 8 + 8, :] = plane_row(state, metric, plane, 0, 8)
        down[plane * 8 : plane * 8 + 8, :] = plane_row(state, metric, plane, 8, 8)
    at = PLANES * 8
    up[at : at + 24, :] = from_left[0:24, :]
    up[at + 24 : at + 48, :] = from_right[0:24, :]
    down[at : at + 24, :] = from_left[24:48, :]
    down[at + 24 : at + 48, :] = from_right[24:48, :]


def next_col(centre, halo, lane):
    edge = lane == 0
    return (
        pltpu.roll(jnp.where(edge, halo, centre), LANES - 1, 1),
        pltpu.roll(jnp.where(edge, centre, halo), LANES - 1, 1),
    )


def prev_col(centre, halo, lane):
    edge = lane == LANES - 1
    return pltpu.roll(jnp.where(edge, halo, centre), 1, 1), pltpu.roll(jnp.where(edge, centre, halo), 1, 1)


EXT = ROWS + 2 * HALO


def advance_kernel(state, metric, from_left, from_right, from_up, from_down, out, wide, terrain):
    gx = lax.axis_index("gx")
    gy = lax.axis_index("gy")
    lane8 = iota((8, LANES), 1)
    at = PLANES * 8

    def unpack(ref_left, left_at, ref_right, right_at, plane):
        group, s = divmod(plane, 16)
        right_part = pltpu.roll(ref_right[right_at + 8 * group : right_at + 8 * group + 8, :], (LANES - 8 * s) % LANES, 1)
        left_part = pltpu.roll(ref_left[left_at + 8 * group : left_at + 8 * group + 8, :], (120 - 8 * s) % LANES, 1)
        return jnp.where(lane8 < 8, right_part, jnp.where(lane8 >= 120, left_part, 0.0))

    def store(plane, row, centre, halo):
        if plane < 4 * L:
            wide[plane, 0, row : row + 8, :] = centre
            wide[plane, 1, row : row + 8, :] = halo
        else:
            terrain[plane - 4 * L, 0, row : row + 8, :] = centre
            terrain[plane - 4 * L, 1, row : row + 8, :] = halo

    for plane in range(PLANES):
        store(plane, 0, from_up[plane * 8 : plane * 8 + 8, :], unpack(from_up, at, from_up, at + 24, plane))
        for rt in range(2):
            store(
                plane,
                8 + 8 * rt,
                plane_row(state, metric, plane, rt * 8, 8),
                unpack(from_left, 24 * rt, from_right, 24 * rt, plane),
            )
        store(plane, 24, from_down[plane * 8 : plane * 8 + 8, :], unpack(from_down, at, from_down, at + 24, plane))

    row = iota((EXT, LANES), 0) + ROWS * gx - HALO
    lane = iota((EXT, LANES), 1)
    row_in = (row >= 0) & (row < N_X)
    last = lax.axis_size("gy") - 1
    halo_in = row_in & (((lane < 8) & (gy < last)) | ((lane >= 120) & (gy > 0)))
    for tile, inside in ((0, row_in), (1, halo_in)):
        inverse = 1.0 / jnp.where(inside, terrain[2, tile], 1.0)
        terrain[2, tile] = inverse
        terrain[3, tile] = jnp.where(inside, 0.5, 0.0)

    def substep(_, carry):
        for k in range(L):
            up, low = min(k + 1, L - 1), max(k - 1, 0)
            sigma = 1.0 - (k + 0.5) / L
            centre, halo = wide[24 + k, 0], wide[24 + k, 1]
            east = next_col(centre, halo, lane)
            west = prev_col(centre, halo, lane)
            for tile in range(2):
                here = (centre, halo)[tile]
                step = terrain[3, tile]
                press_z = (wide[24 + up, tile] - wide[24 + low, tile]) * (0.5 * terrain[2, tile])
                grad_x = (pltpu.roll(here, EXT - 1, 0) - pltpu.roll(here, 1, 0)) * 0.5
                grad_y = (east[tile] - west[tile]) * 0.5
                lean = sigma * press_z
                wide[k, tile] = wide[k, tile] - step * (grad_x - terrain[0, tile] * lean)
                wide[8 + k, tile] = wide[8 + k, tile] - step * (grad_y - terrain[1, tile] * lean)
                wide[16 + k, tile] = wide[16 + k, tile] - 0.5 * press_z
        for k in range(L):
            up, low = min(k + 1, L - 1), max(k - 1, 0)
            sigma = 1.0 - (k + 0.5) / L
            north = next_col(wide[8 + k, 0], wide[8 + k, 1], lane)
            south = prev_col(wide[8 + k, 0], wide[8 + k, 1], lane)
            for tile in range(2):
                wind = wide[k, tile]
                flat = pltpu.roll(wind, EXT - 1, 0) - pltpu.roll(wind, 1, 0) + north[tile] - south[tile]
                slope = terrain[0, tile] * (wide[up, tile] - wide[low, tile])
                slope = slope + terrain[1, tile] * (wide[8 + up, tile] - wide[8 + low, tile])
                rise = wide[16 + up, tile] - wide[16 + low, tile]
                spread = 0.5 * (flat + terrain[2, tile] * (rise - sigma * slope))
                wide[24 + k, tile] = wide[24 + k, tile] - terrain[3, tile] * spread
        return carry

    lax.fori_loop(0, SUB, substep, 0)
    for plane in range(4 * L):
        out[plane * ROWS : plane * ROWS + ROWS, :] = wide[plane, 0, HALO : HALO + ROWS, :]


def spread_kernel(got, placement, slots):
    nest = jnp.minimum(lax.axis_index("gx"), NESTS - 1)
    ox, oy = placement[nest, 0], placement[nest, 1]

    def rows_of(first):
        parts = []
        for a in range(2):
            start = ((first + a) // ROWS) * SLOT + a * 24
            parts.append(got[pl.ds(pl.multiple_of(start, 8), 24), :])
        return jnp.concatenate(parts, 0)

    west, east = rows_of(ox), rows_of(ox + EAST)
    lane = iota((X_ROWS, LANES), 1)
    fine = iota((16, LANES), 1) % ROWS
    for q in range(8):
        shift = (oy + (LANES * q) // R) % LANES
        left = pltpu.roll(west, (LANES - shift) % LANES, 1)
        right = pltpu.roll(east, (LANES + 64 - shift) % LANES, 1)
        slots[q * SLOT : q * SLOT + X_ROWS, :] = jnp.where(lane < 64, left, right)
        start = ox + (ROWS * q) // R
        low = start // ROWS
        high = jnp.minimum(low + 1, 7)
        near = got[pl.ds(pl.multiple_of(low * SLOT + X_ROWS, 8), 16), :]
        far = got[pl.ds(pl.multiple_of(high * SLOT + X_ROWS, 8), 16), :]
        slots[q * SLOT + X_ROWS : q * SLOT + SLOT, :] = jnp.where(fine >= start % ROWS, near, far)


def merge_kernel(got, placement, across, south, north):
    nest = jnp.minimum(lax.axis_index("gx"), NESTS - 1)
    oy = placement[nest, 1]
    start = oy + (LANES * lax.axis_index("gy")) // R
    low = start // LANES
    high = jnp.minimum(low + 1, 7)
    near = got[pl.ds(pl.multiple_of(low * SLOT, 8), X_ROWS), :]
    far = got[pl.ds(pl.multiple_of(high * SLOT, 8), X_ROWS), :]
    lane = iota((X_ROWS, LANES), 1) % 64
    across[...] = jnp.where(lane < LANES * (low + 1) - start, near, far)

    def columns(col):
        return got[pl.ds(pl.multiple_of((col // LANES) * SLOT + X_ROWS, 8), 16), :]

    which = iota((16, LANES), 0) % 3
    south[...] = jnp.where(which == 0, columns(oy), columns(oy + 1))
    top = oy + NORTH
    north[...] = jnp.where(which == 0, columns(top), jnp.where(which == 1, columns(top + 1), columns(top + 2)))


def third(value):
    return (value * 171) >> 9


def relax_kernel(moved, west, east, south, north, placement, zones, out):
    group = lax.axis_index("nest")
    gx = lax.axis_index("gx")
    gy = lax.axis_index("gy")
    nest = jnp.minimum(group, NESTS - 1)
    ox = placement[nest, 0]
    last_x, last_y = lax.axis_size("gx") - 1, lax.axis_size("gy") - 1
    source = jnp.where(gx == 0, west[...], east[...])
    lane = iota((X_ROWS, LANES), 1)
    phase = (LANES * gy) % R
    index = third(lane + phase) + jnp.where(gx == 0, 0, 64)
    across = jnp.take_along_axis(source, index, axis=1)

    big_row, big_lane = iota((LANES, LANES), 0), iota((LANES, LANES), 1)
    parent_row = (ox + third(ROWS * gx + big_row % ROWS)) % ROWS
    pick = ((big_row // ROWS == big_lane // ROWS) & (big_lane % ROWS == parent_row)).astype(F32)

    row, col = iota((ROWS, LANES), 0), iota((ROWS, LANES), 1)
    row_pos, col_pos = (row + ROWS * gx).astype(F32), (col + LANES * gy).astype(F32)
    weight = jnp.zeros((ROWS, LANES), F32)
    for edge, dist in enumerate((row_pos, N_X - 1 - row_pos, col_pos, N_Y - 1 - col_pos)):
        width = zones[nest, edge].astype(F32)
        weight = jnp.maximum(weight, jnp.maximum((width - dist) / width, 0.0))
    weight = jnp.where(group < NESTS, weight, 0.0)
    in_x = ((gx == 0) & (row < W_MAX)) | ((gx == last_x) & (row >= ROWS - W_MAX))
    split = jnp.where(gx == 0, 3, ROWS - 2)

    for c, field in enumerate((0, 1, 3)):
        s0, s1 = south[3 * c : 3 * c + 1, :], south[3 * c + 1 : 3 * c + 2, :]
        n0, n1, n2 = (north[3 * c + b : 3 * c + b + 1, :] for b in range(3))
        none = jnp.zeros((1, LANES), F32)
        table = jnp.concatenate(
            [s0, s0, s0, s1, s1, none, none, none, jnp.zeros((112, LANES), F32), none, none, none, n0, n1, n1, n1, n2], 0
        )
        along = lax.dot_general(pick, table, (((1,), (1,)), ((), ())), precision=HIGH, preferred_element_type=F32)
        for k in range(L):
            plane = c * L + k
            line0 = jnp.broadcast_to(across[plane : plane + 1, :], (ROWS, LANES))
            line1 = jnp.broadcast_to(across[24 + plane : 25 + plane, :], (ROWS, LANES))
            target = jnp.where(in_x, jnp.where(row < split, line0, line1), along[k * ROWS : k * ROWS + ROWS, :])
            at = (field * L + k) * ROWS
            value = moved[at : at + ROWS, :]
            out[at : at + ROWS, :] = value + weight * (target - value)
    out[2 * L * ROWS : 3 * L * ROWS, :] = moved[2 * L * ROWS : 3 * L * ROWS, :]


def call(kernel, specs, outs, scratch=()):
    many = tuple(jax.ShapeDtypeStruct(shape, F32) for shape in outs)
    return pl.pallas_call(
        kernel,
        in_specs=list(specs),
        out_specs=tuple(VMEM_SPEC for _ in outs),
        out_shape=many,
        scratch_shapes=list(scratch),
    )


def local(state, metric, placement, zones):
    flat = state.reshape(4 * L * ROWS, LANES)
    ground = metric.reshape(3 * ROWS, LANES)
    V, S = VMEM_SPEC, SMEM_SPEC
    size = lax.axis_size("gx")
    up_pairs = [(i, i + 1) for i in range(size - 1)]
    down_pairs = [(i + 1, i) for i in range(size - 1)]

    slots, left, right = call(pack_kernel, (V, V, S), [(8 * SLOT, LANES), (48, LANES), (48, LANES)])(
        flat, ground, placement
    )
    first = lax.all_to_all(slots.reshape(8, SLOT, LANES), "gx", 0, 0).reshape(8 * SLOT, LANES)
    from_left = lax.ppermute(right, "gy", up_pairs)
    from_right = lax.ppermute(left, "gy", down_pairs)
    ext = PLANES * 8 + 48
    to_up, to_down = call(join_kernel, (V, V, V, V), [(ext, LANES)] * 2)(flat, ground, from_left, from_right)
    from_up = lax.ppermute(to_down, "gx", up_pairs)
    from_down = lax.ppermute(to_up, "gx", down_pairs)
    (second,) = call(spread_kernel, (V, S), [(8 * SLOT, LANES)])(first, placement)
    arrived = lax.all_to_all(second.reshape(8, SLOT, LANES), "gy", 0, 0).reshape(8 * SLOT, LANES)
    (moved,) = call(
        advance_kernel,
        (V,) * 6,
        [(4 * L * ROWS, LANES)],
        [pltpu.VMEM((4 * L, 2, EXT, LANES), F32), pltpu.VMEM((4, 2, EXT, LANES), F32)],
    )(flat, ground, from_left, from_right, from_up, from_down)
    across, south, north = call(merge_kernel, (V, S), [(X_ROWS, LANES), (16, LANES), (16, LANES)])(arrived, placement)
    axes = ("nest", "gx", "gy")

    def send(value, place):
        pairs = []
        for n in range(NESTS):
            for q in range(8):
                x, y = place(q)
                pairs.append(((NESTS * 8 + n) * 8 + q, (n * 8 + x) * 8 + y))
        return lax.ppermute(value, axes, pairs)

    west = send(across, lambda q: (0, q))
    east = send(across, lambda q: (7, q))
    bottom = send(south, lambda q: (q, 0))
    top = send(north, lambda q: (q, 7))
    (result,) = call(relax_kernel, (V,) * 5 + (S, S), [(4 * L * ROWS, LANES)])(
        moved, west, east, bottom, top, placement, zones
    )
    return result.reshape(state.shape)


def solution(mesh):
    return jax.shard_map(
        local,
        mesh=mesh,
        in_specs=(P("nest", None, None, "gx", "gy"), P("nest", None, "gx", "gy"), P(), P()),
        out_specs=P("nest", None, None, "gx", "gy"),
        check_vma=False,
    )
```

time: 867 us -> 69.5 us (0.08)
  the two profiles are of different devices: /device:TPU:1 before, /device:TPU:12 now
where the time goes in v1:
time: 69.5 us; the launch traced here: 68.8 us
  starting transfers between devices  20.3 us (29%)
  blocking collectives  18.1 us (26%)
  Pallas kernels  13.5 us (19%)
  waiting for transfers between devices  11.5 us (17%)
  local copies, waits for them, and re-layouts  5.21 us (7%)
    all_to_all x1, blocking collectives, local(): lax.all_to_all(slots.reshape(8, SLOT, LANES), 'gx', 0, 0)  18.1 us
    ppermute x4, waiting for transfers between devices, send(): return lax.ppermute(value, axes, pairs)  8.62 us
    all_to_all x1, starting transfers between devices, local(): lax.all_to_all(second.reshape(8, SLOT, LANES), 'gy', 0, 0)  7.4 us
    unnamed x26, local copies, waits for them, and re-layouts  5.21 us
    ppermute x1, starting transfers between devices, local(): from_down = lax.ppermute(to_up, 'gx', down_pairs)  3.93 us
    pallas_call x1, Pallas kernels, local(): call(advance_kernel, (V,) * 6, [(4 * L * ROWS, LANES)], [pltpu.VMEM((4 *...  3.88 us
    ppermute x4, starting transfers between devices, send(): return lax.ppermute(value, axes, pairs)  3.4 us
    ppermute x1, waiting for transfers between devices, local(): from_right = lax.ppermute(left, 'gy', down_pairs)  2.91 us
  transfers between devices with their start and end apart: 9, of which 2 were waited for; matrix products, arithmetic and copies ran while one was open for 1% of the time, Pallas kernels for 10%

profile of v1, /device:TPU:12, one launch (start us, length us, event | category | flops | bytes accessed | tf_op | source)
XLA Modules:
  0.0 68.8 jit_solution(13978164530678710155)
XLA Ops:
  0.0 1.3 %copy.5.placement = s32[7,2]{1,0:T(8,128)} copy(s32[7,2]{0,1:T(2,128)} %param.6) | data formatting | bytes 112 | tf_op args[2]
  1.3 2.1 %shard_map.46 = (f32[512,128]{1,0:T(8,128)}, f32[48,128]{1,0:T(8,128)}, f32[48,128]{1,0:T(8,128)}) custom-call(f32[512,128]{1,0:T(8,128)} %bitcast.7, f32[48,128]{1,0:T(8,128)} %bitcast.14, s32[7,2]{1,0:T(8,128)} %copy.5.placement), custom_call_target="tpu_custom_call" | custom-call | tf_op jit(solution)/shard_map/pallas_call | solution.py:304
  3.5 18.1 %all_to_all.10 = f32[8,64,128]{2,1,0:T(8,128)} all-to-all(f32[8,64,128]{2,1,0:T(8,128)} %bitcast.13), channel_id=1, replica_groups=mesh['nest'=8,'gx'=8,'gy'=8] {'gx'}, dimensions={0} | all-to-all | bytes 524288 | tf_op jit(solution)/shard_map/all_to_all | solution.py:307
  21.6 1.9 %shard_map.49 = f32[512,128]{1,0:T(8,128)} custom-call(f32[512,128]{1,0:T(8,128)} %bitcast.12, s32[7,2]{1,0:T(8,128)} %copy.5.placement), custom_call_target="tpu_custom_call" | custom-call | tf_op jit(solution)/shard_map/pallas_call | solution.py:314
  23.5 7.4 %all-to-all-start.1 = ((f32[8,64,128]{2,1,0:T(8,128)}), f32[8,64,128]{2,1,0:T(8,128)S(1)}, u32[]{:S(2)}, u32[]{:S(2)}) async-start(f32[8,64,128]{2,1,0:T(8,128)} %bitcast.11), calls=%async_computation.1 | async-start | bytes 524288 | tf_op jit(solution)/shard_map/all_to_all | solution.py:315
  30.9 2.4 %collective-permute-start = (f32[48,128]{1,0:T(8,128)S(1)}, f32[48,128]{1,0:T(8,128)S(1)}, u32[]{:S(2)}, u32[]{:S(2)}) collective-permute-start(f32[48,128]{1,0:T(8,128)S(1)} %copy-done.11), channel_id=1, source_target_pairs={{0,1},{1,2},{2,3},{3,4},{4,5},{5,6},{6,7},{8,9},{9,10},{10,11},{11... | collective-permute-start | bytes 73736 | tf_op jit(solution)/shard_map/ppermute | solution.py:308
  33.3 1.3 %collective-permute-start.1 = (f32[48,128]{1,0:T(8,128)S(1)}, f32[48,128]{1,0:T(8,128)S(1)}, u32[]{:S(2)}, u32[]{:S(2)}) collective-permute-start(f32[48,128]{1,0:T(8,128)S(1)} %copy-done.10), channel_id=1, source_target_pairs={{1,0},{2,1},{3,2},{4,3},{5,4},{6,5},{7,6},{9,8},{10,9},{11,10},{12... | collective-permute-start | bytes 73736 | tf_op jit(solution)/shard_map/ppermute | solution.py:309
  34.6 0.0 collective-permute-done.from_left
  34.6 2.9 %collective-permute-done.1.from_right = f32[48,128]{1,0:T(8,128)S(1)} collective-permute-done((f32[48,128]{1,0:T(8,128)S(1)}, f32[48,128]{1,0:T(8,128)S(1)}, u32[]{:S(2)}, u32[]{:S(2)}) %collective-permute-start.1) | collective-permute-done | bytes 24608 | tf_op jit(solution)/shard_map/ppermute | solution.py:309
  37.5 0.6 copy-done.4
  38.1 1.7 %shard_map.47 = (f32[328,128]{1,0:T(8,128)}, f32[328,128]{1,0:T(8,128)}) custom-call(f32[512,128]{1,0:T(8,128)} %bitcast.8, f32[48,128]{1,0:T(8,128)} %bitcast.15, f32[48,128]{1,0:T(8,128)} %copy-done.3, f32[48,128]{1,0:T(8,128)} %copy-done.4), custom_call_target="tpu_custom_call" | custom-call | tf_op jit(solution)/shard_map/pallas_call | solution.py:311
  39.9 1.9 %collective-permute-start.2 = (f32[328,128]{1,0:T(8,128)}, f32[328,128]{1,0:T(8,128)S(1)}, u32[]{:S(2)}, u32[]{:S(2)}) collective-permute-start(f32[328,128]{1,0:T(8,128)} %get-tuple-element.15), channel_id=1, source_target_pairs={{0,8},{8,16},{16,24},{24,32},{32,40},{40,48},{48,56},{1,9},{9,17},... | collective-permute-start | bytes 503816 | tf_op jit(solution)/shard_map/ppermute | solution.py:312
  41.8 3.9 %collective-permute-start.3 = (f32[328,128]{1,0:T(8,128)}, f32[328,128]{1,0:T(8,128)S(1)}, u32[]{:S(2)}, u32[]{:S(2)}) collective-permute-start(f32[328,128]{1,0:T(8,128)} %get-tuple-element.16), channel_id=1, source_target_pairs={{8,0},{16,8},{24,16},{32,24},{40,32},{48,40},{56,48},{9,1},{17,9},... | collective-permute-start | bytes 503816 | tf_op jit(solution)/shard_map/ppermute | solution.py:313
  45.7 0.0 all-to-all-done.1
  45.7 0.0 copy-start
  45.7 0.7 %copy-done = f32[8,64,128]{2,1,0:T(8,128)} copy-done((f32[8,64,128]{2,1,0:T(8,128)}, f32[8,64,128]{2,1,0:T(8,128)S(1)}, u32[]{:S(2)}) %copy-start) | copy-done | bytes 262168
  46.4 1.6 %shard_map.50 = (f32[48,128]{1,0:T(8,128)}, f32[16,128]{1,0:T(8,128)}, f32[16,128]{1,0:T(8,128)}) custom-call(f32[512,128]{1,0:T(8,128)} %bitcast.10, s32[7,2]{1,0:T(8,128)} %copy.5.placement), custom_call_target="tpu_custom_call" | custom-call | tf_op jit(solution)/shard_map/pallas_call | solution.py:322
  48.0 0.8 %collective-permute-start.5 = (f32[48,128]{1,0:T(8,128)}, f32[48,128]{1,0:T(8,128)S(1)}, u32[]{:S(2)}, u32[]{:S(2)}) collective-permute-start(f32[48,128]{1,0:T(8,128)} %get-tuple-element.18), channel_id=1, source_target_pairs={{448,56},{449,57},{450,58},{451,59},{452,60},{453,61},{454,62},{45... | collective-permute-start | bytes 73736 | tf_op jit(solution)/shard_map/ppermute | solution.py:331
  48.8 0.7 collective-permute-start.4
  49.5 1.3 %collective-permute-start.6 = (f32[16,128]{1,0:T(8,128)}, f32[16,128]{1,0:T(8,128)S(1)}, u32[]{:S(2)}, u32[]{:S(2)}) collective-permute-start(f32[16,128]{1,0:T(8,128)} %get-tuple-element.19), channel_id=1, source_target_pairs={{448,0},{449,8},{450,16},{451,24},{452,32},{453,40},{454,48},{455,... | collective-permute-start | bytes 24584 | tf_op jit(solution)/shard_map/ppermute | solution.py:331
  50.8 0.0 collective-permute-done.2.from_up
  50.8 0.0 copy-start.1
  50.8 0.7 collective-permute-start.7
  51.5 0.7 copy.9.zones
  52.2 0.7 copy-done.2
  52.9 3.9 %shard_map.48.moved = f32[512,128]{1,0:T(8,128)} custom-call(f32[512,128]{1,0:T(8,128)} %bitcast.9, f32[48,128]{1,0:T(8,128)} %bitcast.16, f32[48,128]{1,0:T(8,128)} %copy-done.3, f32[48,128]{1,0:T(8,128)} %copy-done.4, f32[328,128]{1,0:T(8,128)} %copy-done.1, f32[328,128]{1,0:T(8,128)} %copy-done.2), custom_call_target="tpu_custom_call" | custom-call | tf_op jit(solution)/shard_map/pallas_call | solution.py:316
  56.7 8.6 %collective-permute-done.6.south = f32[16,128]{1,0:T(8,128)S(1)} collective-permute-done((f32[16,128]{1,0:T(8,128)}, f32[16,128]{1,0:T(8,128)S(1)}, u32[]{:S(2)}, u32[]{:S(2)}) %collective-permute-start.6) | collective-permute-done | bytes 8224 | tf_op jit(solution)/shard_map/ppermute | solution.py:331
  65.4 0.6 copy-done.7
  65.9 0.0 copy-done.8
  66.0 0.0 copy-done.5
  66.0 0.6 copy-done.6
  66.6 2.2 %shard_map.51 = f32[512,128]{1,0:T(8,128)} custom-call(f32[512,128]{1,0:T(8,128)} %shard_map.48.moved, f32[48,128]{1,0:T(8,128)} %copy-done.6, f32[48,128]{1,0:T(8,128)} %copy-done.5, f32[16,128]{1,0:T(8,128)} %copy-done.7, f32[16,128]{1,0:T(8,128)} %copy-done.8, s32[7,2]{1,0:T(8,128)} %copy.5.placement, s32[7,4]{1,0:T(8,128)} %copy.9.zones), custom_call_target="tpu_custom_call" | custom-call | tf_op jit(solution)/shard_map/pallas_call | solution.py:337
  (19 shorter events, 0.0 us)
Async XLA Ops:
  23.5 7.4 %copy-start.11 = (f32[48,128]{1,0:T(8,128)S(1)}, f32[48,128]{1,0:T(8,128)}, u32[]{:S(2)}) copy-start(f32[48,128]{1,0:T(8,128)} %get-tuple-element.13) | copy-start | bytes 73732
  23.5 9.8 %copy-start.10 = (f32[48,128]{1,0:T(8,128)S(1)}, f32[48,128]{1,0:T(8,128)}, u32[]{:S(2)}) copy-start(f32[48,128]{1,0:T(8,128)} %get-tuple-element.14) | copy-start | bytes 73732
  23.5 22.2 %all-to-all-start.1 = ((f32[8,64,128]{2,1,0:T(8,128)}), f32[8,64,128]{2,1,0:T(8,128)S(1)}, u32[]{:S(2)}, u32[]{:S(2)}) async-start(f32[8,64,128]{2,1,0:T(8,128)} %bitcast.11), calls=%async_computation.1 | async-start | bytes 524288 | tf_op jit(solution)/shard_map/all_to_all | solution.py:315
  30.9 3.7 %collective-permute-start = (f32[48,128]{1,0:T(8,128)S(1)}, f32[48,128]{1,0:T(8,128)S(1)}, u32[]{:S(2)}, u32[]{:S(2)}) collective-permute-start(f32[48,128]{1,0:T(8,128)S(1)} %copy-done.11), channel_id=1, source_target_pairs={{0,1},{1,2},{2,3},{3,4},{4,5},{5,6},{6,7},{8,9},{9,10},{10,11},{11... | collective-permute-start | bytes 73736 | tf_op jit(solution)/shard_map/ppermute | solution.py:308
  33.3 4.2 %collective-permute-start.1 = (f32[48,128]{1,0:T(8,128)S(1)}, f32[48,128]{1,0:T(8,128)S(1)}, u32[]{:S(2)}, u32[]{:S(2)}) collective-permute-start(f32[48,128]{1,0:T(8,128)S(1)} %copy-done.10), channel_id=1, source_target_pairs={{1,0},{2,1},{3,2},{4,3},{5,4},{6,5},{7,6},{9,8},{10,9},{11,10},{12... | collective-permute-start | bytes 73736 | tf_op jit(solution)/shard_map/ppermute | solution.py:309
  34.6 2.9 %copy-start.3 = (f32[48,128]{1,0:T(8,128)}, f32[48,128]{1,0:T(8,128)S(1)}, u32[]{:S(2)}) copy-start(f32[48,128]{1,0:T(8,128)S(1)} %collective-permute-done.from_left) | copy-start | bytes 73732
  37.5 0.6 copy-start.4
  39.9 10.9 %collective-permute-start.2 = (f32[328,128]{1,0:T(8,128)}, f32[328,128]{1,0:T(8,128)S(1)}, u32[]{:S(2)}, u32[]{:S(2)}) collective-permute-start(f32[328,128]{1,0:T(8,128)} %get-tuple-element.15), channel_id=1, source_target_pairs={{0,8},{8,16},{16,24},{24,32},{32,40},{40,48},{48,56},{1,9},{9,17},... | collective-permute-start | bytes 503816 | tf_op jit(solution)/shard_map/ppermute | solution.py:312
  41.8 10.4 %collective-permute-start.3 = (f32[328,128]{1,0:T(8,128)}, f32[328,128]{1,0:T(8,128)S(1)}, u32[]{:S(2)}, u32[]{:S(2)}) collective-permute-start(f32[328,128]{1,0:T(8,128)} %get-tuple-element.16), channel_id=1, source_target_pairs={{8,0},{16,8},{24,16},{32,24},{40,32},{48,40},{56,48},{9,1},{17,9},... | collective-permute-start | bytes 503816 | tf_op jit(solution)/shard_map/ppermute | solution.py:313
  45.7 0.7 %copy-start = (f32[8,64,128]{2,1,0:T(8,128)}, f32[8,64,128]{2,1,0:T(8,128)S(1)}, u32[]{:S(2)}) copy-start(f32[8,64,128]{2,1,0:T(8,128)S(1)} %all-to-all-done.1) | copy-start | bytes 786436
  48.0 3.5 %copy-start.9 = (s32[7,4]{0,1:T(4,128)S(1)}, s32[7,4]{0,1:T(4,128)}, u32[]{:S(2)}) copy-start(s32[7,4]{0,1:T(4,128)} %param.7) | copy-start | bytes 340
  48.0 17.3 %collective-permute-start.5 = (f32[48,128]{1,0:T(8,128)}, f32[48,128]{1,0:T(8,128)S(1)}, u32[]{:S(2)}, u32[]{:S(2)}) collective-permute-start(f32[48,128]{1,0:T(8,128)} %get-tuple-element.18), channel_id=1, source_target_pairs={{448,56},{449,57},{450,58},{451,59},{452,60},{453,61},{454,62},{45... | collective-permute-start | bytes 73736 | tf_op jit(solution)/shard_map/ppermute | solution.py:331
  48.8 16.5 %collective-permute-start.4 = (f32[48,128]{1,0:T(8,128)}, f32[48,128]{1,0:T(8,128)S(1)}, u32[]{:S(2)}, u32[]{:S(2)}) collective-permute-start(f32[48,128]{1,0:T(8,128)} %get-tuple-element.18), channel_id=1, source_target_pairs={{448,0},{449,1},{450,2},{451,3},{452,4},{453,5},{454,6},{455,7},{4... | collective-permute-start | bytes 73736 | tf_op jit(solution)/shard_map/ppermute | solution.py:331
  49.5 15.8 %collective-permute-start.6 = (f32[16,128]{1,0:T(8,128)}, f32[16,128]{1,0:T(8,128)S(1)}, u32[]{:S(2)}, u32[]{:S(2)}) collective-permute-start(f32[16,128]{1,0:T(8,128)} %get-tuple-element.19), channel_id=1, source_target_pairs={{448,0},{449,8},{450,16},{451,24},{452,32},{453,40},{454,48},{455,... | collective-permute-start | bytes 24584 | tf_op jit(solution)/shard_map/ppermute | solution.py:331
  50.8 1.4 %copy-start.1 = (f32[328,128]{1,0:T(8,128)}, f32[328,128]{1,0:T(8,128)S(1)}, u32[]{:S(2)}) copy-start(f32[328,128]{1,0:T(8,128)S(1)} %collective-permute-done.2.from_up) | copy-start | bytes 503812
  50.8 14.5 %collective-permute-start.7 = (f32[16,128]{1,0:T(8,128)}, f32[16,128]{1,0:T(8,128)S(1)}, u32[]{:S(2)}, u32[]{:S(2)}) collective-permute-start(f32[16,128]{1,0:T(8,128)} %get-tuple-element.20), channel_id=1, source_target_pairs={{448,7},{449,15},{450,23},{451,31},{452,39},{453,47},{454,55},{455... | collective-permute-start | bytes 24584 | tf_op jit(solution)/shard_map/ppermute | solution.py:331
  52.2 0.7 copy-start.2
  65.3 0.6 copy-start.7
  65.4 0.6 copy-start.8
  65.4 0.6 copy-start.5
  66.0 0.6 copy-start.6

commit v2 on v1

v2 whole, which is shorter than its diff:
```python
import jax
import jax.numpy as jnp
from jax import lax
from jax.experimental import pallas as pl
from jax.experimental.pallas import tpu as pltpu
from jax.sharding import PartitionSpec as P


SUB = 4
R = 3
W_MAX = 5
L = 8
NESTS = 7
HALO = 8
ROWS = 16
LANES = 128
PLANES = 4 * L + 3
SLOT = 64
FINE = 32
X_ROWS = 48
THREE = 24
N_X = 128
N_Y = 1024
EAST = (N_X - 1) // R - 1
NORTH = (N_Y - 1) // R - 2
F32 = jnp.float32
HIGH = lax.Precision.HIGHEST

SEAT = (4, 1, 7, 2, 6, 3, 5)

SEAT = (4, 1, 7, 2, 6, 3, 5)
SPARE = 0

VMEM_SPEC = pl.BlockSpec(memory_space=pltpu.VMEM)
SMEM_SPEC = pl.BlockSpec(memory_space=pltpu.SMEM)


def iota(shape, dim):
    return lax.broadcasted_iota(jnp.int32, shape, dim)


def plane_row(state, metric, plane, row, count):
    if plane < 4 * L:
        return state[plane * ROWS + row : plane * ROWS + row + count, :]
    start = (plane - 4 * L) * ROWS + row
    return metric[start : start + count, :]


def select_kernel(state, placement, slots, fields, store, sems, out_sems):
    gx = lax.axis_index("gx")
    gy = lax.axis_index("gy")
    loads = []
    for t, field in enumerate((0, 1, 3)):
        rows = pl.ds(field * L * ROWS, L * ROWS)
        loads.append(pltpu.make_async_copy(state.at[rows], fields.at[pl.ds(t * L * ROWS, L * ROWS)], sems.at[t]))
        loads[-1].start()
    rows_n = iota((THREE, LANES), 0)
    first = jnp.zeros((THREE, LANES), jnp.int32)
    bases = []
    for n in range(NESTS):
        low = placement[0, n] - ROWS * gx
        bases.append(jnp.where((low >= -1) & (low < ROWS), low, low + EAST))
        low = placement[1, n] - LANES * gy
        base = jnp.where((low >= -1) & (low < LANES), low, low + NORTH)
        first = jnp.where((rows_n >= 3 * n) & (rows_n < 3 * n + 3), base + rows_n - 3 * n, first)
    pick = (iota((THREE, LANES), 1) == first).astype(F32)
    for t in range(3):
        loads[t].wait()
        start = t * L * ROWS
        cols = lax.dot_general(
            pick, fields[start : start + 128, :], (((1,), (1,)), ((), ())), precision=HIGH, preferred_element_type=F32
        )
        for n in range(NESTS):
            at = SEAT[n] * SLOT
            for a in range(2):
                row = jnp.clip(bases[n] + a, 0, ROWS - 1)
                out = at + a * THREE + t * L
                store[out : out + L, :] = fields[pl.ds(start + row, L, stride=ROWS), :]
            store[at + X_ROWS + 3 * t : at + X_ROWS + 3 * t + 3, :] = cols[3 * n : 3 * n + 3, :]
    for n in range(8):
        part = pl.ds(n * SLOT, SLOT)
        if n == SPARE:
            store[part, :] = jnp.zeros((SLOT, LANES), F32)
        else:
            store[n * SLOT + X_ROWS + 9 : n * SLOT + SLOT, :] = jnp.zeros((7, LANES), F32)
    whole_copy = pltpu.make_async_copy(store, slots, out_sems.at[0])
    whole_copy.start()
    whole_copy.wait()


def edge_kernel(state, metric, up, down):
    for plane in range(PLANES):
        up[plane * 8 : plane * 8 + 8, :] = plane_row(state, metric, plane, 0, 8)
        down[plane * 8 : plane * 8 + 8, :] = plane_row(state, metric, plane, 8, 8)


def strip(state, metric, from_up, from_down, plane, rt):
    if rt == 0:
        return from_up[plane * 8 : plane * 8 + 8, :]
    if rt == 3:
        return from_down[plane * 8 : plane * 8 + 8, :]
    return plane_row(state, metric, plane, (rt - 1) * 8, 8)


def pack_kernel(state, metric, from_up, from_down, left, right):
    lane = iota((8, LANES), 1) // 8
    for rt in range(4):
        for group in range(3):
            left_sum = jnp.zeros((8, LANES), F32)
            right_sum = jnp.zeros((8, LANES), F32)
            for s in range(16):
                plane = group * 16 + s
                if plane >= PLANES:
                    break
                value = strip(state, metric, from_up, from_down, plane, rt)
                left_sum = jnp.where(lane == s, pltpu.roll(value, 8 * s, 1) if s else value, left_sum)
                shift = (8 * s + 8) % LANES
                right_sum = jnp.where(lane == s, pltpu.roll(value, shift, 1) if shift else value, right_sum)
            at = (rt * 3 + group) * 8
            left[at : at + 8, :] = left_sum
            right[at : at + 8, :] = right_sum


def next_col(centre, halo, lane):
    edge = lane == 0
    return (
        pltpu.roll(jnp.where(edge, halo, centre), LANES - 1, 1),
        pltpu.roll(jnp.where(edge, centre, halo), LANES - 1, 1),
    )


def prev_col(centre, halo, lane):
    edge = lane == LANES - 1
    return pltpu.roll(jnp.where(edge, halo, centre), 1, 1), pltpu.roll(jnp.where(edge, centre, halo), 1, 1)


EXT = ROWS + 2 * HALO


def advance_kernel(state, metric, from_up, from_down, from_left, from_right, out, wide, terrain):
    gx = lax.axis_index("gx")
    gy = lax.axis_index("gy")
    lane8 = iota((8, LANES), 1)
    for plane in range(PLANES):
        group, s = divmod(plane, 16)
        for rt in range(4):
            at = (rt * 3 + group) * 8
            right_part = pltpu.roll(from_right[at : at + 8, :], (LANES - 8 * s) % LANES, 1)
            left_part = pltpu.roll(from_left[at : at + 8, :], (120 - 8 * s) % LANES, 1)
            halo = jnp.where(lane8 < 8, right_part, jnp.where(lane8 >= 120, left_part, 0.0))
            centre = strip(state, metric, from_up, from_down, plane, rt)
            if plane < 4 * L:
                wide[plane, 0, rt * 8 : rt * 8 + 8, :] = centre
                wide[plane, 1, rt * 8 : rt * 8 + 8, :] = halo
            else:
                terrain[plane - 4 * L, 0, rt * 8 : rt * 8 + 8, :] = centre
                terrain[plane - 4 * L, 1, rt * 8 : rt * 8 + 8, :] = halo

    row = iota((EXT, LANES), 0) + ROWS * gx - HALO
    lane = iota((EXT, LANES), 1)
    row_in = (row >= 0) & (row < N_X)
    last = lax.axis_size("gy") - 1
    halo_in = row_in & (((lane < 8) & (gy < last)) | ((lane >= 120) & (gy > 0)))
    for tile, inside in ((0, row_in), (1, halo_in)):
        inverse = 1.0 / jnp.where(inside, terrain[2, tile], 1.0)
        terrain[2, tile] = inverse
        terrain[3, tile] = jnp.where(inside, 0.5, 0.0)

    def substep(_, carry):
        for k in range(L):
            up, low = min(k + 1, L - 1), max(k - 1, 0)
            sigma = 1.0 - (k + 0.5) / L
            centre, halo = wide[24 + k, 0], wide[24 + k, 1]
            east = next_col(centre, halo, lane)
            west = prev_col(centre, halo, lane)
            for tile in range(2):
                here = (centre, halo)[tile]
                step = terrain[3, tile]
                press_z = (wide[24 + up, tile] - wide[24 + low, tile]) * (0.5 * terrain[2, tile])
                grad_x = (pltpu.roll(here, EXT - 1, 0) - pltpu.roll(here, 1, 0)) * 0.5
                grad_y = (east[tile] - west[tile]) * 0.5
                lean = sigma * press_z
                wide[k, tile] = wide[k, tile] - step * (grad_x - terrain[0, tile] * lean)
                wide[8 + k, tile] = wide[8 + k, tile] - step * (grad_y - terrain[1, tile] * lean)
                wide[16 + k, tile] = wide[16 + k, tile] - 0.5 * press_z
        for k in range(L):
            up, low = min(k + 1, L - 1), max(k - 1, 0)
            sigma = 1.0 - (k + 0.5) / L
            north = next_col(wide[8 + k, 0], wide[8 + k, 1], lane)
            south = prev_col(wide[8 + k, 0], wide[8 + k, 1], lane)
            for tile in range(2):
                wind = wide[k, tile]
                flat = pltpu.roll(wind, EXT - 1, 0) - pltpu.roll(wind, 1, 0) + north[tile] - south[tile]
                slope = terrain[0, tile] * (wide[up, tile] - wide[low, tile])
                slope = slope + terrain[1, tile] * (wide[8 + up, tile] - wide[8 + low, tile])
                rise = wide[16 + up, tile] - wide[16 + low, tile]
                spread = 0.5 * (flat + terrain[2, tile] * (rise - sigma * slope))
                wide[24 + k, tile] = wide[24 + k, tile] - terrain[3, tile] * spread
        return carry

    lax.fori_loop(0, SUB, substep, 0)
    for plane in range(4 * L):
        out[plane * ROWS : plane * ROWS + ROWS, :] = wide[plane, 0, HALO : HALO + ROWS, :]


def seated(seat):
    nest = 0
    for n in range(1, NESTS):
        nest = jnp.where(seat == SEAT[n], n, nest)
    return nest


def spread_kernel(got, placement, slots):
    gx = lax.axis_index("gx")
    nest = seated(lax.axis_index("gy"))
    ox, oy = placement[0, nest], placement[1, nest]
    lane = iota((THREE, LANES), 1)

    def line(col, b, c):
        return got[pl.ds((col // LANES) * SLOT + X_ROWS + 3 * c + b, 1), :]

    south = [[line(oy + b, b, c) for c in range(3)] for b in range(2)]
    north = [[line(oy + NORTH + b, b, c) for c in range(3)] for b in range(3)]
    even = jnp.concatenate(south[0] + north[0] + [north[2][0], north[2][2]], 0)
    odd = jnp.concatenate(south[1] + north[1] + [north[2][1], north[2][2]], 0)
    half = iota((8, LANES), 1) % ROWS < 8
    for q in range(8):
        start = oy + (LANES * q) // R
        low = start // LANES
        high = jnp.minimum(low + 1, 7)
        shift = start % LANES
        parts = []
        for a in range(2):
            near = got[pl.ds(pl.multiple_of(low * SLOT + a * THREE, 8), THREE), :]
            far = got[pl.ds(pl.multiple_of(high * SLOT + a * THREE, 8), THREE), :]
            parts.append(pltpu.roll(jnp.where(lane >= shift, near, far), (LANES + 64 * a - shift) % LANES, 1))
        slots[q * FINE : q * FINE + THREE, :] = jnp.where(lane < 64, parts[0], parts[1])
        turn = ROWS * gx - ox - (ROWS * q) // R + 4 * LANES
        slots[q * FINE + THREE : q * FINE + FINE, :] = jnp.where(
            half, pltpu.roll(even, turn % LANES, 1), pltpu.roll(odd, (turn + 8) % LANES, 1)
        )


def merge_kernel(got, placement, west, east, along):
    nest = seated(lax.axis_index("gy"))
    ox = placement[0, nest]
    lane = iota((THREE, LANES), 1)

    def rows(row):
        return got[pl.ds(pl.multiple_of((row // ROWS) * FINE, 8), THREE), :]

    west[...] = jnp.where(lane < 64, rows(ox), rows(ox + 1))
    east[...] = jnp.where(lane < 64, rows(ox + EAST), rows(ox + EAST + 1))
    start = ox + (ROWS * lax.axis_index("gx")) // R
    low = start // ROWS
    high = jnp.minimum(low + 1, 7)
    near = got[pl.ds(pl.multiple_of(low * FINE + THREE, 8), 8), :]
    far = got[pl.ds(pl.multiple_of(high * FINE + THREE, 8), 8), :]
    along[...] = jnp.where(iota((8, LANES), 1) % 8 < ROWS * (low + 1) - start, near, far)


def third(value):
    return (value * 171) >> 9


def relax_kernel(moved, west, east, south, north, placement, zones, out, store, sems):
    group = lax.axis_index("nest")
    gx = lax.axis_index("gx")
    gy = lax.axis_index("gy")
    nest = jnp.minimum(group, NESTS - 1)
    last_x = lax.axis_size("gx") - 1
    size = L * ROWS
    copies = [
        pltpu.make_async_copy((moved if f == 2 else store).at[pl.ds(f * size, size)], out.at[pl.ds(f * size, size)], sems.at[f])
        for f in range(4)
    ]
    copies[2].start()
    source = jnp.where(gx == 0, west[...], east[...])
    index = third(iota((THREE, LANES), 1) + (LANES * gy) % R)
    lines = [jnp.take_along_axis(source, index + 64 * a, axis=1) for a in range(2)]

    big_row, big_lane = iota((LANES, LANES), 0), iota((LANES, LANES), 1)
    need = third(big_row % ROWS + (ROWS * gx) % R)
    pick = ((big_row // ROWS == big_lane // ROWS) & (big_lane % 8 == need)).astype(F32)

    row, col = iota((ROWS, LANES), 0), iota((ROWS, LANES), 1)
    row_pos, col_pos = (row + ROWS * gx).astype(F32), (col + LANES * gy).astype(F32)
    weight = jnp.zeros((ROWS, LANES), F32)
    for edge, dist in enumerate((row_pos, N_X - 1 - row_pos, col_pos, N_Y - 1 - col_pos)):
        width = zones[edge, nest].astype(F32)
        weight = jnp.maximum(weight, jnp.maximum((width - dist) / width, 0.0))
    weight = jnp.where(group < NESTS, weight, 0.0)
    in_x = ((gx == 0) & (row < W_MAX)) | ((gx == last_x) & (row >= ROWS - W_MAX))
    split = jnp.where(gx == 0, 3, ROWS - 2)

    lane8, row8 = iota((8, LANES), 1), iota((8, LANES), 0)
    first_half = lane8 % ROWS < 8
    for c, field in enumerate((0, 1, 3)):
        pair = jnp.broadcast_to(south[c : c + 1, :], (8, LANES))
        low = jnp.where(first_half == (row8 < 3), pair, 0.0)
        low = jnp.where(row8 < W_MAX, low, 0.0)
        pair = jnp.broadcast_to(north[3 + c : 4 + c, :], (8, LANES))
        last = jnp.broadcast_to(north[(6, 6, 7)[c] : (7, 7, 8)[c], :], (8, LANES))
        last = jnp.where(first_half == (c != 1), last, 0.0)
        high = jnp.where(first_half == (row8 < 4), pair, 0.0)
        high = jnp.where(row8 == 7, last, jnp.where(row8 >= 3, high, 0.0))
        table = jnp.concatenate([low, jnp.zeros((112, LANES), F32), high], 0)
        along = lax.dot_general(pick, table, (((1,), (1,)), ((), ())), precision=HIGH, preferred_element_type=F32)
        for k in range(L):
            plane = c * L + k
            line0 = jnp.broadcast_to(lines[0][plane : plane + 1, :], (ROWS, LANES))
            line1 = jnp.broadcast_to(lines[1][plane : plane + 1, :], (ROWS, LANES))
            target = jnp.where(in_x, jnp.where(row < split, line0, line1), along[k * ROWS : k * ROWS + ROWS, :])
            at = (field * L + k) * ROWS
            value = moved[at : at + ROWS, :]
            store[at : at + ROWS, :] = value + weight * (target - value)
        copies[field].start()
    for f in range(4):
        copies[f].wait()


ANY_SPEC = pl.BlockSpec(memory_space=pl.ANY)


def call(kernel, specs, outs, scratch=(), near=True):
    many = tuple(pltpu.VMEM(shape, F32) if near else jax.ShapeDtypeStruct(shape, F32) for shape in outs)
    run = pl.pallas_call(
        kernel,
        in_specs=list(specs),
        out_specs=tuple(VMEM_SPEC if near else ANY_SPEC for _ in outs),
        out_shape=many,
        scratch_shapes=list(scratch),
    )

    def placed(*args):
        return run(*(pltpu.with_memory_space_constraint(a, pltpu.VMEM) if s is VMEM_SPEC else a for a, s in zip(args, specs)))

    return placed


def local(state, metric, placement, zones):
    return whole(state, metric, placement.T, zones.T)


def whole(state, metric, placement, zones):
    flat = state.reshape(4 * L * ROWS, LANES)
    ground = metric.reshape(3 * ROWS, LANES)
    V, S, A = VMEM_SPEC, SMEM_SPEC, ANY_SPEC
    size = lax.axis_size("gx")
    up_pairs = [(i, i + 1) for i in range(size - 1)]
    down_pairs = [(i + 1, i) for i in range(size - 1)]
    axes = ("nest", "gx", "gy")
    DMA = pltpu.SemaphoreType.DMA

    (slots,) = call(
        select_kernel,
        (A, S),
        [(8 * SLOT, LANES)],
        [pltpu.VMEM((3 * L * ROWS, LANES), F32), pltpu.VMEM((8 * SLOT, LANES), F32), DMA((3,)), DMA((1,))],
        near=False,
    )(flat, placement)
    first = lax.all_to_all(slots.reshape(8, SLOT, LANES), "gy", 0, 0).reshape(8 * SLOT, LANES)
    to_up, to_down = call(edge_kernel, (V, V), [(PLANES * 8, LANES)] * 2)(flat, ground)
    from_up = lax.ppermute(to_down, "gx", up_pairs)
    from_down = lax.ppermute(to_up, "gx", down_pairs)
    (second,) = call(spread_kernel, (V, S), [(8 * FINE, LANES)])(first, placement)
    arrived = lax.all_to_all(second.reshape(8, FINE, LANES), "gx", 0, 0).reshape(8 * FINE, LANES)
    left, right = call(pack_kernel, (V,) * 4, [(96, LANES)] * 2)(flat, ground, from_up, from_down)
    from_left = lax.ppermute(right, "gy", up_pairs)
    from_right = lax.ppermute(left, "gy", down_pairs)
    across, beyond, along = call(merge_kernel, (V, S), [(THREE, LANES), (THREE, LANES), (8, LANES)])(arrived, placement)

    def send(value, place):
        pairs = []
        for n in range(NESTS):
            for q in range(8):
                x, y = place(q)
                pairs.append(((NESTS * 8 + q) * 8 + SEAT[n], (n * 8 + x) * 8 + y))
        return lax.ppermute(value, axes, pairs)

    west = send(across, lambda q: (0, q))
    east = send(beyond, lambda q: (7, q))
    top = send(along, lambda q: (q, 7))
    bottom = send(along, lambda q: (q, 0))
    (moved,) = call(
        advance_kernel,
        (V,) * 6,
        [(4 * L * ROWS, LANES)],
        [pltpu.VMEM((4 * L, 2, EXT, LANES), F32), pltpu.VMEM((4, 2, EXT, LANES), F32)],
    )(flat, ground, from_up, from_down, from_left, from_right)
    (result,) = call(
        relax_kernel,
        (V,) * 5 + (S, S),
        [(4 * L * ROWS, LANES)],
        [pltpu.VMEM((4 * L * ROWS, LANES), F32), DMA((4,))],
        near=False,
    )(moved, west, east, bottom, top, placement, zones)
    return result.reshape(state.shape)


def solution(mesh):
    return jax.shard_map(
        local,
        mesh=mesh,
        in_specs=(P("nest", None, None, "gx", "gy"), P("nest", None, "gx", "gy"), P(), P()),
        out_specs=P("nest", None, None, "gx", "gy"),
        check_vma=False,
    )
```

time: 69.5 us -> 64 us (0.921)
  the two profiles are of different devices: /device:TPU:12 before, /device:TPU:24 now
where the time goes in v2:
time: 64 us; the launch traced here: 63.4 us
  starting transfers between devices  19.8 us (31%)
  blocking collectives  17 us (27%)
  waiting for transfers between devices  16.5 us (26%)
  Pallas kernels  9.93 us (16%)
    all_to_all x1, blocking collectives, whole(): lax.all_to_all(slots.reshape(8, SLOT, LANES), 'gy', 0, 0)  17 us
    ppermute x4, waiting for transfers between devices, send(): return lax.ppermute(value, axes, pairs)  10.2 us
    pallas_call x7, Pallas kernels, placed(): run(*(pltpu.with_memory_space_constraint(a, pltpu.VMEM) if s is VMEM_SPEC...  9.93 us
    all_to_all x1, starting transfers between devices, whole(): lax.all_to_all(second.reshape(8, FINE, LANES), 'gx', 0, 0)  7.45 us
    ppermute x1, waiting for transfers between devices, whole(): from_down = lax.ppermute(to_up, 'gx', down_pairs)  5.59 us
    ppermute x1, starting transfers between devices, whole(): from_up = lax.ppermute(to_down, 'gx', up_pairs)  4.58 us
    ppermute x4, starting transfers between devices, send(): return lax.ppermute(value, axes, pairs)  3.28 us
    ppermute x1, starting transfers between devices, whole(): from_down = lax.ppermute(to_up, 'gx', down_pairs)  1.92 us
  transfers between devices with their start and end apart: 9, of which 3 were waited for; matrix products, arithmetic and copies ran while one was open for 0% of the time, Pallas kernels for 5%

profile of v2, /device:TPU:24, one launch (start us, length us, event | category | flops | bytes accessed | tf_op | source)
XLA Modules:
  0.0 63.4 jit_solution(15599824863631491967)
XLA Ops:
  0.0 3.2 %shard_map.49 = f32[512,128]{1,0:T(8,128)} custom-call(f32[512,128]{1,0:T(8,128)} %bitcast.9, s32[2,7]{1,0:T(2,128)} %bitcast.19), custom_call_target="tpu_custom_call" | custom-call | tf_op jit(solution)/shard_map/pallas_call | solution.py:336
  3.2 17.0 %all_to_all.10 = f32[8,64,128]{2,1,0:T(8,128)S(1)} all-to-all(f32[8,64,128]{2,1,0:T(8,128)} %bitcast.18), channel_id=1, replica_groups=mesh['nest'=8,'gx'=8,'gy'=8] {'gy'}, dimensions={0} | all-to-all | bytes 524288 | tf_op jit(solution)/shard_map/all_to_all | solution.py:362
  20.2 0.0 copy-start
  20.2 1.7 %shard_map.50 = f32[256,128]{1,0:T(8,128)} custom-call(f32[512,128]{1,0:T(8,128)S(1)} %bitcast.13, s32[2,7]{1,0:T(2,128)} %bitcast.20), custom_call_target="tpu_custom_call" | custom-call | tf_op jit(solution)/shard_map/pallas_call | solution.py:336
  21.9 0.0 copy-start.1
  21.9 7.4 %all-to-all-start.1 = ((f32[8,32,128]{2,1,0:T(8,128)}), f32[8,32,128]{2,1,0:T(8,128)S(1)}, u32[]{:S(2)}, u32[]{:S(2)}) async-start(f32[8,32,128]{2,1,0:T(8,128)} %bitcast.5), calls=%async_computation.1 | async-start | bytes 262144 | tf_op jit(solution)/shard_map/all_to_all | solution.py:367
  29.3 0.0 copy-done
  29.3 0.0 copy-done.1
  29.4 4.6 %collective-permute-start = (f32[280,128]{1,0:T(8,128)S(1)}, f32[280,128]{1,0:T(8,128)S(1)}, u32[]{:S(2)}, u32[]{:S(2)}) collective-permute-start(f32[280,128]{1,0:T(8,128)S(1)} %get-tuple-element.12), channel_id=1, source_target_pairs={{0,8},{8,16},{16,24},{24,32},{32,40},{40,48},{48,56},{1,9},{9,17},... | collective-permute-start | bytes 430088 | tf_op jit(solution)/shard_map/ppermute | solution.py:364
  34.0 1.9 %collective-permute-start.1 = (f32[280,128]{1,0:T(8,128)S(1)}, f32[280,128]{1,0:T(8,128)S(1)}, u32[]{:S(2)}, u32[]{:S(2)}) collective-permute-start(f32[280,128]{1,0:T(8,128)S(1)} %get-tuple-element.13), channel_id=1, source_target_pairs={{8,0},{16,8},{24,16},{32,24},{40,32},{48,40},{56,48},{9,1},{17,9},... | collective-permute-start | bytes 430088 | tf_op jit(solution)/shard_map/ppermute | solution.py:365
  35.9 0.7 %collective-permute-done.from_up = f32[280,128]{1,0:T(8,128)S(1)} collective-permute-done((f32[280,128]{1,0:T(8,128)S(1)}, f32[280,128]{1,0:T(8,128)S(1)}, u32[]{:S(2)}, u32[]{:S(2)}) %collective-permute-start) | collective-permute-done | bytes 143392 | tf_op jit(solution)/shard_map/ppermute | solution.py:364
  36.6 5.6 %collective-permute-done.1.from_down = f32[280,128]{1,0:T(8,128)S(1)} collective-permute-done((f32[280,128]{1,0:T(8,128)S(1)}, f32[280,128]{1,0:T(8,128)S(1)}, u32[]{:S(2)}, u32[]{:S(2)}) %collective-permute-start.1) | collective-permute-done | bytes 143392 | tf_op jit(solution)/shard_map/ppermute | solution.py:365
  42.2 0.3 shard_map.47
  42.5 1.3 %collective-permute-start.2 = (f32[96,128]{1,0:T(8,128)S(1)}, f32[96,128]{1,0:T(8,128)S(1)}, u32[]{:S(2)}, u32[]{:S(2)}) collective-permute-start(f32[96,128]{1,0:T(8,128)S(1)} %get-tuple-element.14), channel_id=1, source_target_pairs={{0,1},{1,2},{2,3},{3,4},{4,5},{5,6},{6,7},{8,9},{9,10},{10,11},{11... | collective-permute-start | bytes 147464 | tf_op jit(solution)/shard_map/ppermute | solution.py:369
  43.8 1.3 %collective-permute-start.3 = (f32[96,128]{1,0:T(8,128)S(1)}, f32[96,128]{1,0:T(8,128)S(1)}, u32[]{:S(2)}, u32[]{:S(2)}) collective-permute-start(f32[96,128]{1,0:T(8,128)S(1)} %get-tuple-element.15), channel_id=1, source_target_pairs={{1,0},{2,1},{3,2},{4,3},{5,4},{6,5},{7,6},{9,8},{10,9},{11,10},{12... | collective-permute-start | bytes 147464 | tf_op jit(solution)/shard_map/ppermute | solution.py:370
  45.1 0.0 all-to-all-done.1
  45.1 0.7 %shard_map.51 = (f32[24,128]{1,0:T(8,128)S(1)}, f32[24,128]{1,0:T(8,128)S(1)}, f32[8,128]{1,0:T(8,128)S(1)}) custom-call(f32[256,128]{1,0:T(8,128)S(1)} %bitcast.14, s32[2,7]{1,0:T(2,128)} %bitcast.21), custom_call_target="tpu_custom_call" | custom-call | tf_op jit(solution)/shard_map/pallas_call | solution.py:336
  45.9 0.7 %collective-permute-start.4 = (f32[24,128]{1,0:T(8,128)S(1)}, f32[24,128]{1,0:T(8,128)S(1)}, u32[]{:S(2)}, u32[]{:S(2)}) collective-permute-start(f32[24,128]{1,0:T(8,128)S(1)} %get-tuple-element.16), channel_id=1, source_target_pairs={{452,0},{460,1},{468,2},{476,3},{484,4},{492,5},{500,6},{508,7},{4... | collective-permute-start | bytes 36872 | tf_op jit(solution)/shard_map/ppermute | solution.py:379
  46.5 0.7 %collective-permute-start.5 = (f32[24,128]{1,0:T(8,128)S(1)}, f32[24,128]{1,0:T(8,128)S(1)}, u32[]{:S(2)}, u32[]{:S(2)}) collective-permute-start(f32[24,128]{1,0:T(8,128)S(1)} %get-tuple-element.17), channel_id=1, source_target_pairs={{452,56},{460,57},{468,58},{476,59},{484,60},{492,61},{500,62},{50... | collective-permute-start | bytes 36872 | tf_op jit(solution)/shard_map/ppermute | solution.py:379
  47.2 0.7 %collective-permute-start.7 = (f32[8,128]{1,0:T(8,128)S(1)}, f32[8,128]{1,0:T(8,128)S(1)}, u32[]{:S(2)}, u32[]{:S(2)}) collective-permute-start(f32[8,128]{1,0:T(8,128)S(1)} %get-tuple-element.18), channel_id=1, source_target_pairs={{452,7},{460,15},{468,23},{476,31},{484,39},{492,47},{500,55},{508... | collective-permute-start | bytes 12296 | tf_op jit(solution)/shard_map/ppermute | solution.py:379
  47.9 0.0 collective-permute-done.2.from_left
  47.9 1.3 %collective-permute-start.6 = (f32[8,128]{1,0:T(8,128)S(1)}, f32[8,128]{1,0:T(8,128)S(1)}, u32[]{:S(2)}, u32[]{:S(2)}) collective-permute-start(f32[8,128]{1,0:T(8,128)S(1)} %get-tuple-element.18), channel_id=1, source_target_pairs={{452,0},{460,8},{468,16},{476,24},{484,32},{492,40},{500,48},{508,... | collective-permute-start | bytes 12296 | tf_op jit(solution)/shard_map/ppermute | solution.py:379
  49.2 0.0 collective-permute-done.3.from_right
  49.2 2.0 %shard_map.48.moved = f32[512,128]{1,0:T(8,128)S(1)} custom-call(f32[512,128]{1,0:T(8,128)S(1)} %bitcast.12, f32[48,128]{1,0:T(8,128)S(1)} %bitcast.17, f32[280,128]{1,0:T(8,128)S(1)} %collective-permute-done.from_up, f32[280,128]{1,0:T(8,128)S(1)} %collective-permute-done.1.from_down, f32[96,128]{1,0:T(8,128)S(1)} %collective-permute-done.2.from_left, ...), custom_call_target="tpu_custom_call" | custom-call | tf_op jit(solution)/shard_map/pallas_call | solution.py:336
  51.2 0.0 collective-permute-done.7.north
  51.2 10.2 %collective-permute-done.6.south = f32[8,128]{1,0:T(8,128)S(1)} collective-permute-done((f32[8,128]{1,0:T(8,128)S(1)}, f32[8,128]{1,0:T(8,128)S(1)}, u32[]{:S(2)}, u32[]{:S(2)}) %collective-permute-start.6) | collective-permute-done | bytes 4128 | tf_op jit(solution)/shard_map/ppermute | solution.py:379
  61.4 0.0 collective-permute-done.4.west
  61.4 0.0 collective-permute-done.5.east
  61.4 1.9 %shard_map.52 = f32[512,128]{1,0:T(8,128)} custom-call(f32[512,128]{1,0:T(8,128)S(1)} %shard_map.48.moved, f32[24,128]{1,0:T(8,128)S(1)} %collective-permute-done.4.west, f32[24,128]{1,0:T(8,128)S(1)} %collective-permute-done.5.east, f32[8,128]{1,0:T(8,128)S(1)} %collective-permute-done.6.south, f32[8,128]{1,0:T(8,128)S(1)} %collective-permute-done.7.north, ...), custom_call_target="tpu_custom_call" | custom-call | tf_op jit(solution)/shard_map/pallas_call | solution.py:336
  (1 shorter events, 0.0 us)
Async XLA Ops:
  20.2 9.2 %copy-start = (f32[1,4,8,16,128]{4,3,2,1,0:T(8,128)S(1)}, f32[1,4,8,16,128]{4,3,2,1,0:T(8,128)}, u32[]{:S(2)}) copy-start(f32[1,4,8,16,128]{4,3,2,1,0:T(8,128)} %param.4) | copy-start | bytes 786436
  21.9 7.5 %copy-start.1 = (f32[1,3,16,128]{3,2,1,0:T(8,128)S(1)}, f32[1,3,16,128]{3,2,1,0:T(8,128)}, u32[]{:S(2)}) copy-start(f32[1,3,16,128]{3,2,1,0:T(8,128)} %param.5) | copy-start | bytes 73732
  21.9 23.2 %all-to-all-start.1 = ((f32[8,32,128]{2,1,0:T(8,128)}), f32[8,32,128]{2,1,0:T(8,128)S(1)}, u32[]{:S(2)}, u32[]{:S(2)}) async-start(f32[8,32,128]{2,1,0:T(8,128)} %bitcast.5), calls=%async_computation.1 | async-start | bytes 262144 | tf_op jit(solution)/shard_map/all_to_all | solution.py:367
  29.4 7.2 %collective-permute-start = (f32[280,128]{1,0:T(8,128)S(1)}, f32[280,128]{1,0:T(8,128)S(1)}, u32[]{:S(2)}, u32[]{:S(2)}) collective-permute-start(f32[280,128]{1,0:T(8,128)S(1)} %get-tuple-element.12), channel_id=1, source_target_pairs={{0,8},{8,16},{16,24},{24,32},{32,40},{40,48},{48,56},{1,9},{9,17},... | collective-permute-start | bytes 430088 | tf_op jit(solution)/shard_map/ppermute | solution.py:364
  34.0 8.2 %collective-permute-start.1 = (f32[280,128]{1,0:T(8,128)S(1)}, f32[280,128]{1,0:T(8,128)S(1)}, u32[]{:S(2)}, u32[]{:S(2)}) collective-permute-start(f32[280,128]{1,0:T(8,128)S(1)} %get-tuple-element.13), channel_id=1, source_target_pairs={{8,0},{16,8},{24,16},{32,24},{40,32},{48,40},{56,48},{9,1},{17,9},... | collective-permute-start | bytes 430088 | tf_op jit(solution)/shard_map/ppermute | solution.py:365
  42.5 5.4 %collective-permute-start.2 = (f32[96,128]{1,0:T(8,128)S(1)}, f32[96,128]{1,0:T(8,128)S(1)}, u32[]{:S(2)}, u32[]{:S(2)}) collective-permute-start(f32[96,128]{1,0:T(8,128)S(1)} %get-tuple-element.14), channel_id=1, source_target_pairs={{0,1},{1,2},{2,3},{3,4},{4,5},{5,6},{6,7},{8,9},{9,10},{10,11},{11... | collective-permute-start | bytes 147464 | tf_op jit(solution)/shard_map/ppermute | solution.py:369
  43.8 5.4 %collective-permute-start.3 = (f32[96,128]{1,0:T(8,128)S(1)}, f32[96,128]{1,0:T(8,128)S(1)}, u32[]{:S(2)}, u32[]{:S(2)}) collective-permute-start(f32[96,128]{1,0:T(8,128)S(1)} %get-tuple-element.15), channel_id=1, source_target_pairs={{1,0},{2,1},{3,2},{4,3},{5,4},{6,5},{7,6},{9,8},{10,9},{11,10},{12... | collective-permute-start | bytes 147464 | tf_op jit(solution)/shard_map/ppermute | solution.py:370
  45.9 15.6 %collective-permute-start.4 = (f32[24,128]{1,0:T(8,128)S(1)}, f32[24,128]{1,0:T(8,128)S(1)}, u32[]{:S(2)}, u32[]{:S(2)}) collective-permute-start(f32[24,128]{1,0:T(8,128)S(1)} %get-tuple-element.16), channel_id=1, source_target_pairs={{452,0},{460,1},{468,2},{476,3},{484,4},{492,5},{500,6},{508,7},{4... | collective-permute-start | bytes 36872 | tf_op jit(solution)/shard_map/ppermute | solution.py:379
  46.5 14.9 %collective-permute-start.5 = (f32[24,128]{1,0:T(8,128)S(1)}, f32[24,128]{1,0:T(8,128)S(1)}, u32[]{:S(2)}, u32[]{:S(2)}) collective-permute-start(f32[24,128]{1,0:T(8,128)S(1)} %get-tuple-element.17), channel_id=1, source_target_pairs={{452,56},{460,57},{468,58},{476,59},{484,60},{492,61},{500,62},{50... | collective-permute-start | bytes 36872 | tf_op jit(solution)/shard_map/ppermute | solution.py:379
  47.2 4.0 %collective-permute-start.7 = (f32[8,128]{1,0:T(8,128)S(1)}, f32[8,128]{1,0:T(8,128)S(1)}, u32[]{:S(2)}, u32[]{:S(2)}) collective-permute-start(f32[8,128]{1,0:T(8,128)S(1)} %get-tuple-element.18), channel_id=1, source_target_pairs={{452,7},{460,15},{468,23},{476,31},{484,39},{492,47},{500,55},{508... | collective-permute-start | bytes 12296 | tf_op jit(solution)/shard_map/ppermute | solution.py:379
  47.9 13.6 %collective-permute-start.6 = (f32[8,128]{1,0:T(8,128)S(1)}, f32[8,128]{1,0:T(8,128)S(1)}, u32[]{:S(2)}, u32[]{:S(2)}) collective-permute-start(f32[8,128]{1,0:T(8,128)S(1)} %get-tuple-element.18), channel_id=1, source_target_pairs={{452,0},{460,8},{468,16},{476,24},{484,32},{492,40},{500,48},{508,... | collective-permute-start | bytes 12296 | tf_op jit(solution)/shard_map/ppermute | solution.py:379

commit v3 on v2

--- a/solution.py
+++ b/solution.py
@@ -28,11 +28,23 @@
 
 SEAT = (4, 1, 7, 2, 6, 3, 5)
 
-SEAT = (4, 1, 7, 2, 6, 3, 5)
+SEAT = (6, 3, 7, 2, 5, 1, 4)
 SPARE = 0
 
+
+def ring(a, b):
+    return min((a - b) % 8, (b - a) % 8)
+
+
+def pieces_of(n):
+    far = sorted(range(8), key=lambda q: -ring(4 + SEAT[n] // 2, 4 * (n % 2) + q // 2))
+    near = sorted(range(8), key=lambda g: max(ring(g, 0), ring(g, 7)))
+    return tuple(q for _, q in sorted(zip(near, far)))
+
+
+PIECE = tuple(pieces_of(n) for n in range(NESTS))
+
 VMEM_SPEC = pl.BlockSpec(memory_space=pltpu.VMEM)
-SMEM_SPEC = pl.BlockSpec(memory_space=pltpu.SMEM)
 
 
 def iota(shape, dim):
@@ -46,14 +58,17 @@
     return metric[start : start + count, :]
 
 
-def select_kernel(state, placement, slots, fields, store, sems, out_sems):
+def select_kernel(state, where, slots, info, fields, store, placement, sems, out_sems):
     gx = lax.axis_index("gx")
     gy = lax.axis_index("gy")
+    ask = pltpu.make_async_copy(where, placement, sems.at[3])
+    ask.start()
     loads = []
     for t, field in enumerate((0, 1, 3)):
         rows = pl.ds(field * L * ROWS, L * ROWS)
         loads.append(pltpu.make_async_copy(state.at[rows], fields.at[pl.ds(t * L * ROWS, L * ROWS)], sems.at[t]))
         loads[-1].start()
+    ask.wait()
     rows_n = iota((THREE, LANES), 0)
     first = jnp.zeros((THREE, LANES), jnp.int32)
     bases = []
@@ -64,34 +79,51 @@
         base = jnp.where((low >= -1) & (low < LANES), low, low + NORTH)
         first = jnp.where((rows_n >= 3 * n) & (rows_n < 3 * n + 3), base + rows_n - 3 * n, first)
     pick = (iota((THREE, LANES), 1) == first).astype(F32)
+    store[SPARE] = jnp.zeros((SLOT, LANES), F32)
     for t in range(3):
         loads[t].wait()
+        start = t * L * ROWS
+        for n in range(NESTS):
+            for a in range(2):
+                row = jnp.clip(bases[n] + a, 0, ROWS - 1)
+                out = a * THREE + t * L
+                store[SEAT[n], out : out + L, :] = fields[pl.ds(start + row, L, stride=ROWS), :]
+    lower = pltpu.make_async_copy(store.at[:, 0:X_ROWS], slots.at[:, 0:X_ROWS], out_sems.at[0])
+    lower.start()
+    line, spot = iota((8, LANES), 0), iota((8, LANES), 1)
+    kept = jnp.zeros((8, LANES), F32)
+    for n in range(NESTS):
+        pair = jnp.where(line == 0, placement[0, n], placement[1, n]).astype(F32)
+        kept = jnp.where(spot == n, pair, kept)
+    info[...] = kept
+    for t in range(3):
         start = t * L * ROWS
         cols = lax.dot_general(
             pick, fields[start : start + 128, :], (((1,), (1,)), ((), ())), precision=HIGH, preferred_element_type=F32
         )
         for n in range(NESTS):
-            at = SEAT[n] * SLOT
-            for a in range(2):
-                row = jnp.clip(bases[n] + a, 0, ROWS - 1)
-                out = at + a * THREE + t * L
-                store[out : out + L, :] = fields[pl.ds(start + row, L, stride=ROWS), :]
-            store[at + X_ROWS + 3 * t : at + X_ROWS + 3 * t + 3, :] = cols[3 * n : 3 * n + 3, :]
-    for n in range(8):
-        part = pl.ds(n * SLOT, SLOT)
-        if n == SPARE:
-            store[part, :] = jnp.zeros((SLOT, LANES), F32)
-        else:
-            store[n * SLOT + X_ROWS + 9 : n * SLOT + SLOT, :] = jnp.zeros((7, LANES), F32)
-    whole_copy = pltpu.make_async_copy(store, slots, out_sems.at[0])
-    whole_copy.start()
-    whole_copy.wait()
+            store[SEAT[n], X_ROWS + 3 * t : X_ROWS + 3 * t + 3, :] = cols[3 * n : 3 * n + 3, :]
+    for n in range(NESTS):
+        store[SEAT[n], X_ROWS + 9 : SLOT, :] = jnp.zeros((7, LANES), F32)
+    upper = pltpu.make_async_copy(store.at[:, X_ROWS:SLOT], slots.at[:, X_ROWS:SLOT], out_sems.at[1])
+    upper.start()
+    lower.wait()
+    upper.wait()
 
 
 def edge_kernel(state, metric, up, down):
     for plane in range(PLANES):
         up[plane * 8 : plane * 8 + 8, :] = plane_row(state, metric, plane, 0, 8)
         down[plane * 8 : plane * 8 + 8, :] = plane_row(state, metric, plane, 8, 8)
+
+
+def fetch_kernel(state, metric, from_up, from_down, copy, ground, above, below, sems):
+    pairs = ((state, copy), (metric, ground), (from_up, above), (from_down, below))
+    copies = [pltpu.make_async_copy(a, b, sems.at[i]) for i, (a, b) in enumerate(pairs)]
+    for one in copies:
+        one.start()
+    for one in copies:
+        one.wait()
 
 
 def strip(state, metric, from_up, from_down, plane, rt):
@@ -210,10 +242,17 @@
     return nest
 
 
-def spread_kernel(got, placement, slots):
+def corner(placement, nest):
+    both = placement[...]
+    mine = iota(both.shape, 1) == nest
+    one = [jnp.sum(jnp.where(mine & (iota(both.shape, 0) == d), both, 0.0)) for d in range(2)]
+    return one[0].astype(jnp.int32), one[1].astype(jnp.int32)
+
+
+def spread_kernel(got, placement, slots, store, sems):
     gx = lax.axis_index("gx")
     nest = seated(lax.axis_index("gy"))
-    ox, oy = placement[0, nest], placement[1, nest]
+    ox, oy = corner(placement, nest)
     lane = iota((THREE, LANES), 1)
 
     def line(col, b, c):
@@ -224,8 +263,15 @@
     even = jnp.concatenate(south[0] + north[0] + [north[2][0], north[2][2]], 0)
     odd = jnp.concatenate(south[1] + north[1] + [north[2][1], north[2][2]], 0)
     half = iota((8, LANES), 1) % ROWS < 8
-    for q in range(8):
-        start = oy + (LANES * q) // R
+    copies = [
+        pltpu.make_async_copy(store.at[pl.ds(h * 4 * FINE, 4 * FINE)], slots.at[pl.ds(h * 4 * FINE, 4 * FINE)], sems.at[h])
+        for h in range(2)
+    ]
+    for g in range(8):
+        reach = 0
+        for n in range(NESTS):
+            reach = jnp.where(nest == n, (LANES * PIECE[n][g]) // R, reach)
+        start = oy + reach
         low = start // LANES
         high = jnp.minimum(low + 1, 7)
         shift = start % LANES
@@ -234,16 +280,20 @@
             near = got[pl.ds(pl.multiple_of(low * SLOT + a * THREE, 8), THREE), :]
             far = got[pl.ds(pl.multiple_of(high * SLOT + a * THREE, 8), THREE), :]
             parts.append(pltpu.roll(jnp.where(lane >= shift, near, far), (LANES + 64 * a - shift) % LANES, 1))
-        slots[q * FINE : q * FINE + THREE, :] = jnp.where(lane < 64, parts[0], parts[1])
-        turn = ROWS * gx - ox - (ROWS * q) // R + 4 * LANES
-        slots[q * FINE + THREE : q * FINE + FINE, :] = jnp.where(
+        store[g * FINE : g * FINE + THREE, :] = jnp.where(lane < 64, parts[0], parts[1])
+        turn = ROWS * gx - ox - (ROWS * g) // R + 4 * LANES
+        store[g * FINE + THREE : g * FINE + FINE, :] = jnp.where(
             half, pltpu.roll(even, turn % LANES, 1), pltpu.roll(odd, (turn + 8) % LANES, 1)
         )
+        if g % 4 == 3:
+            copies[g // 4].start()
+    for h in range(2):
+        copies[h].wait()
 
 
 def merge_kernel(got, placement, west, east, along):
     nest = seated(lax.axis_index("gy"))
-    ox = placement[0, nest]
+    ox, _ = corner(placement, nest)
     lane = iota((THREE, LANES), 1)
 
     def rows(row):
@@ -263,7 +313,7 @@
     return (value * 171) >> 9
 
 
-def relax_kernel(moved, west, east, south, north, placement, zones, out, store, sems):
+def relax_kernel(moved, west, east, south, north, zones, out, store, sems):
     group = lax.axis_index("nest")
     gx = lax.axis_index("gx")
     gy = lax.axis_index("gy")
@@ -285,9 +335,11 @@
 
     row, col = iota((ROWS, LANES), 0), iota((ROWS, LANES), 1)
     row_pos, col_pos = (row + ROWS * gx).astype(F32), (col + LANES * gy).astype(F32)
+    own = jnp.where(iota((4, NESTS), 1) == nest, zones[...].astype(F32), 0.0)
+    widths = jnp.sum(own, axis=1, keepdims=True)
     weight = jnp.zeros((ROWS, LANES), F32)
     for edge, dist in enumerate((row_pos, N_X - 1 - row_pos, col_pos, N_Y - 1 - col_pos)):
-        width = zones[edge, nest].astype(F32)
+        width = jnp.broadcast_to(widths[edge : edge + 1, :], (ROWS, LANES))
         weight = jnp.maximum(weight, jnp.maximum((width - dist) / width, 0.0))
     weight = jnp.where(group < NESTS, weight, 0.0)
     in_x = ((gx == 0) & (row < W_MAX)) | ((gx == last_x) & (row >= ROWS - W_MAX))
@@ -323,17 +375,18 @@
 
 
 def call(kernel, specs, outs, scratch=(), near=True):
-    many = tuple(pltpu.VMEM(shape, F32) if near else jax.ShapeDtypeStruct(shape, F32) for shape in outs)
+    places = near if isinstance(near, tuple) else (near,) * len(outs)
+    many = tuple(pltpu.VMEM(shape, F32) if near_by else jax.ShapeDtypeStruct(shape, F32) for shape, near_by in zip(outs, places))
     run = pl.pallas_call(
         kernel,
         in_specs=list(specs),
-        out_specs=tuple(VMEM_SPEC if near else ANY_SPEC for _ in outs),
+        out_specs=tuple(VMEM_SPEC if near_by else ANY_SPEC for near_by in places),
         out_shape=many,
         scratch_shapes=list(scratch),
     )
 
     def placed(*args):
-        return run(*(pltpu.with_memory_space_constraint(a, pltpu.VMEM) if s is VMEM_SPEC else a for a, s in zip(args, specs)))
+        return run(*(a if s is ANY_SPEC else pltpu.with_memory_space_constraint(a, s.memory_space) for a, s in zip(args, specs)))
 
     return placed
 
@@ -345,43 +398,90 @@
 def whole(state, metric, placement, zones):
     flat = state.reshape(4 * L * ROWS, LANES)
     ground = metric.reshape(3 * ROWS, LANES)
-    V, S, A = VMEM_SPEC, SMEM_SPEC, ANY_SPEC
-    size = lax.axis_size("gx")
-    up_pairs = [(i, i + 1) for i in range(size - 1)]
-    down_pairs = [(i + 1, i) for i in range(size - 1)]
+    V, A = VMEM_SPEC, ANY_SPEC
     axes = ("nest", "gx", "gy")
     DMA = pltpu.SemaphoreType.DMA
 
-    (slots,) = call(
-        select_kernel,
-        (A, S),
-        [(8 * SLOT, LANES)],
-        [pltpu.VMEM((3 * L * ROWS, LANES), F32), pltpu.VMEM((8 * SLOT, LANES), F32), DMA((3,)), DMA((1,))],
-        near=False,
-    )(flat, placement)
-    first = lax.all_to_all(slots.reshape(8, SLOT, LANES), "gy", 0, 0).reshape(8 * SLOT, LANES)
-    to_up, to_down = call(edge_kernel, (V, V), [(PLANES * 8, LANES)] * 2)(flat, ground)
-    from_up = lax.ppermute(to_down, "gx", up_pairs)
-    from_down = lax.ppermute(to_up, "gx", down_pairs)
-    (second,) = call(spread_kernel, (V, S), [(8 * FINE, LANES)])(first, placement)
-    arrived = lax.all_to_all(second.reshape(8, FINE, LANES), "gx", 0, 0).reshape(8 * FINE, LANES)
-    left, right = call(pack_kernel, (V,) * 4, [(96, LANES)] * 2)(flat, ground, from_up, from_down)
-    from_left = lax.ppermute(right, "gy", up_pairs)
-    from_right = lax.ppermute(left, "gy", down_pairs)
-    across, beyond, along = call(merge_kernel, (V, S), [(THREE, LANES), (THREE, LANES), (8, LANES)])(arrived, placement)
+    def pairs_of(axis, step, groups):
+        pairs = []
+        for n in groups:
+            for x in range(8):
+                for y in range(8):
+                    to = (x + step, y) if axis == 0 else (x, y + step)
+                    if 0 <= to[axis] < 8:
+                        pairs.append(((n * 8 + x) * 8 + y, (n * 8 + to[0]) * 8 + to[1]))
+        return pairs
+
+    def shifted(value, axis, step, groups):
+        return lax.ppermute(value, axes, pairs_of(axis, step, groups))
+
+    def rows_halo(flat, ground, groups):
+        to_up, to_down = call(edge_kernel, (V, V), [(PLANES * 8, LANES)] * 2)(flat, ground)
+        return shifted(to_down, 0, 1, groups), shifted(to_up, 0, -1, groups)
+
+    def packed(flat, ground, from_up, from_down):
+        return call(pack_kernel, (V,) * 4, [(96, LANES)] * 2)(flat, ground, from_up, from_down)
+
+    def as_parent(flat, ground, placement):
+        mine = (NESTS,)
+        slots, info = call(
+            select_kernel,
+            (A, A),
+            [(8, SLOT, LANES), (8, LANES)],
+            [
+                pltpu.VMEM((3 * L * ROWS, LANES), F32),
+                pltpu.VMEM((8, SLOT, LANES), F32),
+                pltpu.SMEM((2, NESTS), jnp.int32),
+                DMA((4,)),
+                DMA((2,)),
+            ],
+            near=(False, True),
+        )(flat, pltpu.with_memory_space_constraint(placement, pltpu.HBM))
+        first = lax.all_to_all(slots, "gy", 0, 0).reshape(8 * SLOT, LANES)
+        from_up, from_down = rows_halo(flat, ground, mine)
+        (second,) = call(
+            spread_kernel,
+            (V, V),
+            [(8 * FINE, LANES)],
+            [pltpu.VMEM((8 * FINE, LANES), F32), DMA((2,))],
+            near=False,
+        )(first, info)
+        arrived = lax.all_to_all(second.reshape(8, FINE, LANES), "gx", 0, 0).reshape(8 * FINE, LANES)
+        left, right = packed(flat, ground, from_up, from_down)
+        parts = call(merge_kernel, (V, V), [(THREE, LANES), (THREE, LANES), (8, LANES)])(arrived, info)
+        return (from_up, from_down, left, right, *parts)
+
+    def as_nest(flat, ground, placement):
+        others = range(NESTS)
+        from_up, from_down = rows_halo(flat, ground, others)
+        left, right = packed(flat, ground, from_up, from_down)
+        none = jnp.zeros((THREE, LANES), F32)
+        return from_up, from_down, left, right, none, none, none[:8]
+
+    from_up, from_down, left, right, across, beyond, along = lax.cond(
+        lax.axis_index("nest") == NESTS, as_parent, as_nest, flat, ground, placement
+    )
 
     def send(value, place):
         pairs = []
         for n in range(NESTS):
-            for q in range(8):
-                x, y = place(q)
-                pairs.append(((NESTS * 8 + q) * 8 + SEAT[n], (n * 8 + x) * 8 + y))
+            for g in range(8):
+                x, y = place(g, PIECE[n][g])
+                pairs.append(((NESTS * 8 + g) * 8 + SEAT[n], (n * 8 + x) * 8 + y))
         return lax.ppermute(value, axes, pairs)
 
-    west = send(across, lambda q: (0, q))
-    east = send(beyond, lambda q: (7, q))
-    top = send(along, lambda q: (q, 7))
-    bottom = send(along, lambda q: (q, 0))
+    west = send(across, lambda g, q: (0, q))
+    east = send(beyond, lambda g, q: (7, q))
+    top = send(along, lambda g, q: (g, 7))
+    bottom = send(along, lambda g, q: (g, 0))
+    everyone = range(NESTS + 1)
+    from_left, from_right = shifted(right, 1, 1, everyone), shifted(left, 1, -1, everyone)
+    flat, ground, from_up, from_down = call(
+        fetch_kernel,
+        (A,) * 4,
+        [(4 * L * ROWS, LANES), (3 * ROWS, LANES), (PLANES * 8, LANES), (PLANES * 8, LANES)],
+        [DMA((4,))],
+    )(flat, ground, from_up, from_down)
     (moved,) = call(
         advance_kernel,
         (V,) * 6,
@@ -390,11 +490,11 @@
     )(flat, ground, from_up, from_down, from_left, from_right)
     (result,) = call(
         relax_kernel,
-        (V,) * 5 + (S, S),
+        (V,) * 6,
         [(4 * L * ROWS, LANES)],
         [pltpu.VMEM((4 * L * ROWS, LANES), F32), DMA((4,))],
         near=False,
-    )(moved, west, east, bottom, top, placement, zones)
+    )(moved, west, east, bottom, top, zones)
     return result.reshape(state.shape)
 
 

time: 64 us -> 62.9 us (0.983)
  the two profiles are of different devices: /device:TPU:24 before, /device:TPU:56 now
where the time goes in v3:
time: 62.9 us; the launch traced here: 62.3 us
  waiting for transfers between devices  41.8 us (66%)
  starting transfers between devices  13 us (21%)
  Pallas kernels  5.66 us (9%)
  local copies, waits for them, and re-layouts  1.7 us (3%)
    ppermute x4, waiting for transfers between devices, send(): return lax.ppermute(value, axes, pairs)  39.8 us
    ppermute x4, starting transfers between devices, shifted(): return lax.ppermute(value, axes, pairs_of(axis, step, groups))  9.1 us
    pallas_call x5, Pallas kernels, placed(): run(*(a if s is ANY_SPEC else pltpu.with_memory_space_constraint(a, s.mem...  5.66 us
    ppermute x4, starting transfers between devices, send(): return lax.ppermute(value, axes, pairs)  3.91 us
    ppermute x4, waiting for transfers between devices, shifted(): return lax.ppermute(value, axes, pairs_of(axis, step, groups))  2.06 us
    cond x4, local copies, waits for them, and re-layouts  1.69 us
  transfers between devices with their start and end apart: 8, of which 4 were waited for; matrix products, arithmetic and copies ran while one was open for 0% of the time, Pallas kernels for 5%

profile of v3, /device:TPU:56, one launch (start us, length us, event | category | flops | bytes accessed | tf_op | source)
XLA Modules:
  0.0 62.3 jit_solution(7710034087817680165)
XLA Ops:
  0.0 11.6 %conditional.1 = (f32[280,128]{1,0:T(8,128)S(1)}, f32[280,128]{1,0:T(8,128)}, f32[96,128]{1,0:T(8,128)S(1)}, f32[96,128]{1,0:T(8,128)S(1)}, f32[24,128]{1,0:T(8,...) conditional(s32[]{:T(128)} %convert_element_type.3, (f32[512,128]{1,0:T(8,128)}, ...), branch_computations={%region_0.0_spmd, %region_1.0_spmd} | conditional | bytes 4358424 | solution.py:461
  0.0 0.0 copy-start
  0.0 0.9 %copy-done = f32[512,128]{1,0:T(8,128)S(1)} copy-done((f32[512,128]{1,0:T(8,128)S(1)}, f32[512,128]{1,0:T(8,128)}, u32[]{:S(2)}) %copy-start) | copy-done | bytes 262168 | tf_op jit(solution)/shard_map/cond
  1.0 0.0 copy-start.4
  1.0 0.7 %copy-done.4 = f32[48,128]{1,0:T(8,128)S(1)} copy-done((f32[48,128]{1,0:T(8,128)S(1)}, f32[48,128]{1,0:T(8,128)}, u32[]{:S(2)}) %copy-start.4) | copy-done | bytes 24600 | tf_op jit(solution)/shard_map/cond
  1.7 1.3 %collective-permute-start = (f32[280,128]{1,0:T(8,128)S(1)}, f32[280,128]{1,0:T(8,128)S(1)}, u32[]{:S(2)}, u32[]{:S(2)}) collective-permute-start(f32[280,128]{1,0:T(8,128)S(1)} %get-tuple-element.17), channel_id=1, source_target_pairs={{0,8},{1,9},{2,10},{3,11},{4,12},{5,13},{6,14},{7,15},{8,16},{9,17... | collective-permute-start | bytes 430088 | tf_op jit(solution)/shard_map/cond/branch_0_fun/ppermute | solution.py:416
  3.0 5.2 %collective-permute-start.1 = (f32[280,128]{1,0:T(8,128)S(1)}, f32[280,128]{1,0:T(8,128)}, u32[]{:S(2)}, u32[]{:S(2)}) collective-permute-start(f32[280,128]{1,0:T(8,128)S(1)} %get-tuple-element.18), channel_id=1, source_target_pairs={{8,0},{9,1},{10,2},{11,3},{12,4},{13,5},{14,6},{15,7},{16,8},{17,9... | collective-permute-start | bytes 430088 | tf_op jit(solution)/shard_map/cond/branch_0_fun/ppermute | solution.py:416
  8.2 0.9 %collective-permute-done.from_up = f32[280,128]{1,0:T(8,128)S(1)} collective-permute-done((f32[280,128]{1,0:T(8,128)S(1)}, f32[280,128]{1,0:T(8,128)S(1)}, u32[]{:S(2)}, u32[]{:S(2)}) %collective-permute-start) | collective-permute-done | bytes 143392 | tf_op jit(solution)/shard_map/cond/branch_0_fun/ppermute | solution.py:416
  9.1 1.2 %collective-permute-done.1.from_down = f32[280,128]{1,0:T(8,128)} collective-permute-done((f32[280,128]{1,0:T(8,128)S(1)}, f32[280,128]{1,0:T(8,128)}, u32[]{:S(2)}, u32[]{:S(2)}) %collective-permute-start.1) | collective-permute-done | bytes 143392 | tf_op jit(solution)/shard_map/cond/branch_0_fun/ppermute | solution.py:416
  10.3 1.2 %branch_0_fun.3 = (f32[96,128]{1,0:T(8,128)S(1)}, f32[96,128]{1,0:T(8,128)S(1)}) custom-call(f32[512,128]{1,0:T(8,128)S(1)} %copy-done, f32[48,128]{1,0:T(8,128)S(1)} %copy-done.4, f32[280,128]{1,0:T(8,128)S(1)} %collective-permute-done.from_up, f32[280,128]{1,0:T(8,128)} %collective-permute-done.1.from_down), custom_call_target="tpu_custom_call" | custom-call | tf_op jit(solution)/shard_map/cond/branch_0_fun/pallas_call | solution.py:389
  11.6 1.3 %collective-permute-start.4 = (f32[96,128]{1,0:T(8,128)S(1)}, f32[96,128]{1,0:T(8,128)S(1)}, u32[]{:S(2)}, u32[]{:S(2)}) collective-permute-start(f32[96,128]{1,0:T(8,128)S(1)} %get-tuple-element.50), channel_id=1, source_target_pairs={{0,1},{1,2},{2,3},{3,4},{4,5},{5,6},{6,7},{8,9},{9,10},{10,11},{11... | collective-permute-start | bytes 147464 | tf_op jit(solution)/shard_map/ppermute | solution.py:416
  12.9 1.3 %collective-permute-start.5 = (f32[96,128]{1,0:T(8,128)S(1)}, f32[96,128]{1,0:T(8,128)S(1)}, u32[]{:S(2)}, u32[]{:S(2)}) collective-permute-start(f32[96,128]{1,0:T(8,128)S(1)} %get-tuple-element.51), channel_id=1, source_target_pairs={{1,0},{2,1},{3,2},{4,3},{5,4},{6,5},{7,6},{9,8},{10,9},{11,10},{12... | collective-permute-start | bytes 147464 | tf_op jit(solution)/shard_map/ppermute | solution.py:416
  14.2 0.7 %collective-permute-start.6 = (f32[24,128]{1,0:T(8,128)S(1)}, f32[24,128]{1,0:T(8,128)S(1)}, u32[]{:S(2)}, u32[]{:S(2)}) collective-permute-start(f32[24,128]{1,0:T(8,128)S(1)} %get-tuple-element.52), channel_id=1, source_target_pairs={{454,6},{462,4},{470,2},{478,0},{486,1},{494,3},{502,5},{510,7},{4... | collective-permute-start | bytes 36872 | tf_op jit(solution)/shard_map/ppermute | solution.py:471
  14.8 1.3 %collective-permute-start.7 = (f32[24,128]{1,0:T(8,128)S(1)}, f32[24,128]{1,0:T(8,128)S(1)}, u32[]{:S(2)}, u32[]{:S(2)}) collective-permute-start(f32[24,128]{1,0:T(8,128)S(1)} %get-tuple-element.53), channel_id=1, source_target_pairs={{454,62},{462,60},{470,58},{478,56},{486,57},{494,59},{502,61},{51... | collective-permute-start | bytes 36872 | tf_op jit(solution)/shard_map/ppermute | solution.py:471
  16.1 1.3 %collective-permute-start.8 = (f32[8,128]{1,0:T(8,128)S(1)}, f32[8,128]{1,0:T(8,128)S(1)}, u32[]{:S(2)}, u32[]{:S(2)}) collective-permute-start(f32[8,128]{1,0:T(8,128)S(1)} %get-tuple-element.54), channel_id=1, source_target_pairs={{454,0},{462,8},{470,16},{478,24},{486,32},{494,40},{502,48},{510,... | collective-permute-start | bytes 12296 | tf_op jit(solution)/shard_map/ppermute | solution.py:471
  17.4 0.0 collective-permute-done.4.from_left
  17.5 0.7 %collective-permute-start.9 = (f32[8,128]{1,0:T(8,128)S(1)}, f32[8,128]{1,0:T(8,128)S(1)}, u32[]{:S(2)}, u32[]{:S(2)}) collective-permute-start(f32[8,128]{1,0:T(8,128)S(1)} %get-tuple-element.54), channel_id=1, source_target_pairs={{454,7},{462,15},{470,23},{478,31},{486,39},{494,47},{502,55},{510... | collective-permute-start | bytes 12296 | tf_op jit(solution)/shard_map/ppermute | solution.py:471
  18.1 1.2 %shard_map.46 = (f32[512,128]{1,0:T(8,128)S(1)}, f32[48,128]{1,0:T(8,128)S(1)}, f32[280,128]{1,0:T(8,128)S(1)}, f32[280,128]{1,0:T(8,128)S(1)}) custom-call(f32[512,128]{1,0:T(8,128)} %bitcast.10, f32[48,128]{1,0:T(8,128)} %bitcast.14, f32[280,128]{1,0:T(8,128)S(1)} %get-tuple-element.44.from_up, f32[280,128]{1,0:T(8,128)} %get-tuple-element.45.from_down), custom_call_target="tpu_custom_call" | custom-call | tf_op jit(solution)/shard_map/pallas_call | solution.py:389
  19.3 0.0 collective-permute-done.5.from_right
  19.3 0.0 copy-start.6
  19.3 2.0 %shard_map.47.moved = f32[512,128]{1,0:T(8,128)S(1)} custom-call(f32[512,128]{1,0:T(8,128)S(1)} %get-tuple-element.46.state, f32[48,128]{1,0:T(8,128)S(1)} %get-tuple-element.47.metric, f32[280,128]{1,0:T(8,128)S(1)} %get-tuple-element.48.from_up, f32[280,128]{1,0:T(8,128)S(1)} %get-tuple-element.49.from_down, ...), custom_call_target="tpu_custom_call" | custom-call | tf_op jit(solution)/shard_map/pallas_call | solution.py:389
  21.3 34.2 %collective-permute-done.8.south = f32[8,128]{1,0:T(8,128)S(1)} collective-permute-done((f32[8,128]{1,0:T(8,128)S(1)}, f32[8,128]{1,0:T(8,128)S(1)}, u32[]{:S(2)}, u32[]{:S(2)}) %collective-permute-start.8) | collective-permute-done | bytes 4128 | tf_op jit(solution)/shard_map/ppermute | solution.py:471
  55.5 0.0 collective-permute-done.9.north
  55.5 0.0 collective-permute-done.6.west
  55.5 5.6 %collective-permute-done.7.east = f32[24,128]{1,0:T(8,128)S(1)} collective-permute-done((f32[24,128]{1,0:T(8,128)S(1)}, f32[24,128]{1,0:T(8,128)S(1)}, u32[]{:S(2)}, u32[]{:S(2)}) %collective-permute-start.7) | collective-permute-done | bytes 12320 | tf_op jit(solution)/shard_map/ppermute | solution.py:471
  61.1 0.0 copy-done.6
  61.1 1.2 %shard_map.48 = f32[512,128]{1,0:T(8,128)} custom-call(f32[512,128]{1,0:T(8,128)S(1)} %shard_map.47.moved, f32[24,128]{1,0:T(8,128)S(1)} %collective-permute-done.6.west, f32[24,128]{1,0:T(8,128)S(1)} %collective-permute-done.7.east, f32[8,128]{1,0:T(8,128)S(1)} %collective-permute-done.8.south, f32[8,128]{1,0:T(8,128)S(1)} %collective-permute-done.9.north, ...), custom_call_target="tpu_custom_call" | custom-call | tf_op jit(solution)/shard_map/pallas_call | solution.py:389
  (4 shorter events, 0.0 us)
Async XLA Ops:
  0.0 0.9 %copy-start = (f32[512,128]{1,0:T(8,128)S(1)}, f32[512,128]{1,0:T(8,128)}, u32[]{:S(2)}) copy-start(f32[512,128]{1,0:T(8,128)} %get-tuple-element.15.state) | copy-start | bytes 786436 | tf_op jit(solution)/shard_map/cond
  1.0 0.7 %copy-start.4 = (f32[48,128]{1,0:T(8,128)S(1)}, f32[48,128]{1,0:T(8,128)}, u32[]{:S(2)}) copy-start(f32[48,128]{1,0:T(8,128)} %get-tuple-element.16.metric) | copy-start | bytes 73732 | tf_op jit(solution)/shard_map/cond
  1.7 7.4 %collective-permute-start = (f32[280,128]{1,0:T(8,128)S(1)}, f32[280,128]{1,0:T(8,128)S(1)}, u32[]{:S(2)}, u32[]{:S(2)}) collective-permute-start(f32[280,128]{1,0:T(8,128)S(1)} %get-tuple-element.17), channel_id=1, source_target_pairs={{0,8},{1,9},{2,10},{3,11},{4,12},{5,13},{6,14},{7,15},{8,16},{9,17... | collective-permute-start | bytes 430088 | tf_op jit(solution)/shard_map/cond/branch_0_fun/ppermute | solution.py:416
  3.0 7.3 %collective-permute-start.1 = (f32[280,128]{1,0:T(8,128)S(1)}, f32[280,128]{1,0:T(8,128)}, u32[]{:S(2)}, u32[]{:S(2)}) collective-permute-start(f32[280,128]{1,0:T(8,128)S(1)} %get-tuple-element.18), channel_id=1, source_target_pairs={{8,0},{9,1},{10,2},{11,3},{12,4},{13,5},{14,6},{15,7},{16,8},{17,9... | collective-permute-start | bytes 430088 | tf_op jit(solution)/shard_map/cond/branch_0_fun/ppermute | solution.py:416
  11.6 5.9 %collective-permute-start.4 = (f32[96,128]{1,0:T(8,128)S(1)}, f32[96,128]{1,0:T(8,128)S(1)}, u32[]{:S(2)}, u32[]{:S(2)}) collective-permute-start(f32[96,128]{1,0:T(8,128)S(1)} %get-tuple-element.50), channel_id=1, source_target_pairs={{0,1},{1,2},{2,3},{3,4},{4,5},{5,6},{6,7},{8,9},{9,10},{10,11},{11... | collective-permute-start | bytes 147464 | tf_op jit(solution)/shard_map/ppermute | solution.py:416
  12.9 6.4 %collective-permute-start.5 = (f32[96,128]{1,0:T(8,128)S(1)}, f32[96,128]{1,0:T(8,128)S(1)}, u32[]{:S(2)}, u32[]{:S(2)}) collective-permute-start(f32[96,128]{1,0:T(8,128)S(1)} %get-tuple-element.51), channel_id=1, source_target_pairs={{1,0},{2,1},{3,2},{4,3},{5,4},{6,5},{7,6},{9,8},{10,9},{11,10},{12... | collective-permute-start | bytes 147464 | tf_op jit(solution)/shard_map/ppermute | solution.py:416
  14.2 41.4 %collective-permute-start.6 = (f32[24,128]{1,0:T(8,128)S(1)}, f32[24,128]{1,0:T(8,128)S(1)}, u32[]{:S(2)}, u32[]{:S(2)}) collective-permute-start(f32[24,128]{1,0:T(8,128)S(1)} %get-tuple-element.52), channel_id=1, source_target_pairs={{454,6},{462,4},{470,2},{478,0},{486,1},{494,3},{502,5},{510,7},{4... | collective-permute-start | bytes 36872 | tf_op jit(solution)/shard_map/ppermute | solution.py:471
  14.8 46.3 %collective-permute-start.7 = (f32[24,128]{1,0:T(8,128)S(1)}, f32[24,128]{1,0:T(8,128)S(1)}, u32[]{:S(2)}, u32[]{:S(2)}) collective-permute-start(f32[24,128]{1,0:T(8,128)S(1)} %get-tuple-element.53), channel_id=1, source_target_pairs={{454,62},{462,60},{470,58},{478,56},{486,57},{494,59},{502,61},{51... | collective-permute-start | bytes 36872 | tf_op jit(solution)/shard_map/ppermute | solution.py:471
  16.1 39.4 %collective-permute-start.8 = (f32[8,128]{1,0:T(8,128)S(1)}, f32[8,128]{1,0:T(8,128)S(1)}, u32[]{:S(2)}, u32[]{:S(2)}) collective-permute-start(f32[8,128]{1,0:T(8,128)S(1)} %get-tuple-element.54), channel_id=1, source_target_pairs={{454,0},{462,8},{470,16},{478,24},{486,32},{494,40},{502,48},{510,... | collective-permute-start | bytes 12296 | tf_op jit(solution)/shard_map/ppermute | solution.py:471
  17.5 38.1 %collective-permute-start.9 = (f32[8,128]{1,0:T(8,128)S(1)}, f32[8,128]{1,0:T(8,128)S(1)}, u32[]{:S(2)}, u32[]{:S(2)}) collective-permute-start(f32[8,128]{1,0:T(8,128)S(1)} %get-tuple-element.54), channel_id=1, source_target_pairs={{454,7},{462,15},{470,23},{478,31},{486,39},{494,47},{502,55},{510... | collective-permute-start | bytes 12296 | tf_op jit(solution)/shard_map/ppermute | solution.py:471
  19.3 41.8 %copy-start.6 = (s32[7,4]{0,1:T(4,128)S(1)}, s32[7,4]{0,1:T(4,128)}, u32[]{:S(2)}) copy-start(s32[7,4]{0,1:T(4,128)} %param.9) | copy-start | bytes 340

commit v4 on v3

--- a/solution.py
+++ b/solution.py
@@ -28,7 +28,7 @@
 
 SEAT = (4, 1, 7, 2, 6, 3, 5)
 
-SEAT = (6, 3, 7, 2, 5, 1, 4)
+SEAT = (7, 1, 5, 2, 3, 6, 4)
 SPARE = 0
 
 
@@ -117,9 +117,8 @@
         down[plane * 8 : plane * 8 + 8, :] = plane_row(state, metric, plane, 8, 8)
 
 
-def fetch_kernel(state, metric, from_up, from_down, copy, ground, above, below, sems):
-    pairs = ((state, copy), (metric, ground), (from_up, above), (from_down, below))
-    copies = [pltpu.make_async_copy(a, b, sems.at[i]) for i, (a, b) in enumerate(pairs)]
+def fetch_kernel(state, metric, fields, ground, sems):
+    copies = [pltpu.make_async_copy(a, b, sems.at[i]) for i, (a, b) in enumerate(((state, fields), (metric, ground)))]
     for one in copies:
         one.start()
     for one in copies:
@@ -134,7 +133,9 @@
     return plane_row(state, metric, plane, (rt - 1) * 8, 8)
 
 
-def pack_kernel(state, metric, from_up, from_down, left, right):
+def pack_kernel(state, metric, from_up, from_down, left, right, above, below):
+    above[...] = from_up[...]
+    below[...] = from_down[...]
     lane = iota((8, LANES), 1) // 8
     for rt in range(4):
         for group in range(3):
@@ -324,51 +325,60 @@
         pltpu.make_async_copy((moved if f == 2 else store).at[pl.ds(f * size, size)], out.at[pl.ds(f * size, size)], sems.at[f])
         for f in range(4)
     ]
-    copies[2].start()
-    source = jnp.where(gx == 0, west[...], east[...])
-    index = third(iota((THREE, LANES), 1) + (LANES * gy) % R)
-    lines = [jnp.take_along_axis(source, index + 64 * a, axis=1) for a in range(2)]
-
-    big_row, big_lane = iota((LANES, LANES), 0), iota((LANES, LANES), 1)
-    need = third(big_row % ROWS + (ROWS * gx) % R)
-    pick = ((big_row // ROWS == big_lane // ROWS) & (big_lane % 8 == need)).astype(F32)
-
-    row, col = iota((ROWS, LANES), 0), iota((ROWS, LANES), 1)
-    row_pos, col_pos = (row + ROWS * gx).astype(F32), (col + LANES * gy).astype(F32)
-    own = jnp.where(iota((4, NESTS), 1) == nest, zones[...].astype(F32), 0.0)
-    widths = jnp.sum(own, axis=1, keepdims=True)
-    weight = jnp.zeros((ROWS, LANES), F32)
-    for edge, dist in enumerate((row_pos, N_X - 1 - row_pos, col_pos, N_Y - 1 - col_pos)):
-        width = jnp.broadcast_to(widths[edge : edge + 1, :], (ROWS, LANES))
-        weight = jnp.maximum(weight, jnp.maximum((width - dist) / width, 0.0))
-    weight = jnp.where(group < NESTS, weight, 0.0)
-    in_x = ((gx == 0) & (row < W_MAX)) | ((gx == last_x) & (row >= ROWS - W_MAX))
-    split = jnp.where(gx == 0, 3, ROWS - 2)
-
-    lane8, row8 = iota((8, LANES), 1), iota((8, LANES), 0)
-    first_half = lane8 % ROWS < 8
-    for c, field in enumerate((0, 1, 3)):
-        pair = jnp.broadcast_to(south[c : c + 1, :], (8, LANES))
-        low = jnp.where(first_half == (row8 < 3), pair, 0.0)
-        low = jnp.where(row8 < W_MAX, low, 0.0)
-        pair = jnp.broadcast_to(north[3 + c : 4 + c, :], (8, LANES))
-        last = jnp.broadcast_to(north[(6, 6, 7)[c] : (7, 7, 8)[c], :], (8, LANES))
-        last = jnp.where(first_half == (c != 1), last, 0.0)
-        high = jnp.where(first_half == (row8 < 4), pair, 0.0)
-        high = jnp.where(row8 == 7, last, jnp.where(row8 >= 3, high, 0.0))
-        table = jnp.concatenate([low, jnp.zeros((112, LANES), F32), high], 0)
-        along = lax.dot_general(pick, table, (((1,), (1,)), ((), ())), precision=HIGH, preferred_element_type=F32)
-        for k in range(L):
-            plane = c * L + k
-            line0 = jnp.broadcast_to(lines[0][plane : plane + 1, :], (ROWS, LANES))
-            line1 = jnp.broadcast_to(lines[1][plane : plane + 1, :], (ROWS, LANES))
-            target = jnp.where(in_x, jnp.where(row < split, line0, line1), along[k * ROWS : k * ROWS + ROWS, :])
-            at = (field * L + k) * ROWS
-            value = moved[at : at + ROWS, :]
-            store[at : at + ROWS, :] = value + weight * (target - value)
-        copies[field].start()
-    for f in range(4):
-        copies[f].wait()
+
+    @pl.when(group == NESTS)
+    def _():
+        plain = pltpu.make_async_copy(moved, out, sems.at[0])
+        plain.start()
+        plain.wait()
+
+    @pl.when(group < NESTS)
+    def _():
+        copies[2].start()
+        source = jnp.where(gx == 0, west[...], east[...])
+        index = third(iota((THREE, LANES), 1) + (LANES * gy) % R)
+        lines = [jnp.take_along_axis(source, index + 64 * a, axis=1) for a in range(2)]
+
+        big_row, big_lane = iota((LANES, LANES), 0), iota((LANES, LANES), 1)
+        need = third(big_row % ROWS + (ROWS * gx) % R)
+        pick = ((big_row // ROWS == big_lane // ROWS) & (big_lane % 8 == need)).astype(F32)
+
+        row, col = iota((ROWS, LANES), 0), iota((ROWS, LANES), 1)
+        row_pos, col_pos = (row + ROWS * gx).astype(F32), (col + LANES * gy).astype(F32)
+        own = jnp.where(iota((4, NESTS), 1) == nest, zones[...].astype(F32), 0.0)
+        widths = jnp.sum(own, axis=1, keepdims=True)
+        weight = jnp.zeros((ROWS, LANES), F32)
+        for edge, dist in enumerate((row_pos, N_X - 1 - row_pos, col_pos, N_Y - 1 - col_pos)):
+            width = jnp.broadcast_to(widths[edge : edge + 1, :], (ROWS, LANES))
+            weight = jnp.maximum(weight, jnp.maximum((width - dist) / width, 0.0))
+        weight = jnp.where(group < NESTS, weight, 0.0)
+        in_x = ((gx == 0) & (row < W_MAX)) | ((gx == last_x) & (row >= ROWS - W_MAX))
+        split = jnp.where(gx == 0, 3, ROWS - 2)
+
+        lane8, row8 = iota((8, LANES), 1), iota((8, LANES), 0)
+        first_half = lane8 % ROWS < 8
+        for c, field in enumerate((0, 1, 3)):
+            pair = jnp.broadcast_to(south[c : c + 1, :], (8, LANES))
+            low = jnp.where(first_half == (row8 < 3), pair, 0.0)
+            low = jnp.where(row8 < W_MAX, low, 0.0)
+            pair = jnp.broadcast_to(north[3 + c : 4 + c, :], (8, LANES))
+            last = jnp.broadcast_to(north[(6, 6, 7)[c] : (7, 7, 8)[c], :], (8, LANES))
+            last = jnp.where(first_half == (c != 1), last, 0.0)
+            high = jnp.where(first_half == (row8 < 4), pair, 0.0)
+            high = jnp.where(row8 == 7, last, jnp.where(row8 >= 3, high, 0.0))
+            table = jnp.concatenate([low, jnp.zeros((112, LANES), F32), high], 0)
+            along = lax.dot_general(pick, table, (((1,), (1,)), ((), ())), precision=HIGH, preferred_element_type=F32)
+            for k in range(L):
+                plane = c * L + k
+                line0 = jnp.broadcast_to(lines[0][plane : plane + 1, :], (ROWS, LANES))
+                line1 = jnp.broadcast_to(lines[1][plane : plane + 1, :], (ROWS, LANES))
+                target = jnp.where(in_x, jnp.where(row < split, line0, line1), along[k * ROWS : k * ROWS + ROWS, :])
+                at = (field * L + k) * ROWS
+                value = moved[at : at + ROWS, :]
+                store[at : at + ROWS, :] = value + weight * (target - value)
+            copies[field].start()
+        for f in range(4):
+            copies[f].wait()
 
 
 ANY_SPEC = pl.BlockSpec(memory_space=pl.ANY)
@@ -420,7 +430,9 @@
         return shifted(to_down, 0, 1, groups), shifted(to_up, 0, -1, groups)
 
     def packed(flat, ground, from_up, from_down):
-        return call(pack_kernel, (V,) * 4, [(96, LANES)] * 2)(flat, ground, from_up, from_down)
+        return call(pack_kernel, (V,) * 4, [(96, LANES)] * 2 + [(PLANES * 8, LANES)] * 2)(
+            flat, ground, from_up, from_down
+        )
 
     def as_parent(flat, ground, placement):
         mine = (NESTS,)
@@ -447,16 +459,16 @@
             near=False,
         )(first, info)
         arrived = lax.all_to_all(second.reshape(8, FINE, LANES), "gx", 0, 0).reshape(8 * FINE, LANES)
-        left, right = packed(flat, ground, from_up, from_down)
+        left, right, above, below = packed(flat, ground, from_up, from_down)
         parts = call(merge_kernel, (V, V), [(THREE, LANES), (THREE, LANES), (8, LANES)])(arrived, info)
-        return (from_up, from_down, left, right, *parts)
+        return (above, below, left, right, *parts)
 
     def as_nest(flat, ground, placement):
         others = range(NESTS)
         from_up, from_down = rows_halo(flat, ground, others)
-        left, right = packed(flat, ground, from_up, from_down)
+        left, right, above, below = packed(flat, ground, from_up, from_down)
         none = jnp.zeros((THREE, LANES), F32)
-        return from_up, from_down, left, right, none, none, none[:8]
+        return above, below, left, right, none, none, none[:8]
 
     from_up, from_down, left, right, across, beyond, along = lax.cond(
         lax.axis_index("nest") == NESTS, as_parent, as_nest, flat, ground, placement
@@ -476,12 +488,7 @@
     bottom = send(along, lambda g, q: (g, 0))
     everyone = range(NESTS + 1)
     from_left, from_right = shifted(right, 1, 1, everyone), shifted(left, 1, -1, everyone)
-    flat, ground, from_up, from_down = call(
-        fetch_kernel,
-        (A,) * 4,
-        [(4 * L * ROWS, LANES), (3 * ROWS, LANES), (PLANES * 8, LANES), (PLANES * 8, LANES)],
-        [DMA((4,))],
-    )(flat, ground, from_up, from_down)
+    flat, ground = call(fetch_kernel, (A, A), [(4 * L * ROWS, LANES), (3 * ROWS, LANES)], [DMA((2,))])(flat, ground)
     (moved,) = call(
         advance_kernel,
         (V,) * 6,

time: 62.9 us -> 59.7 us (0.949)
  the two profiles are of different devices: /device:TPU:56 before, /device:TPU:58 now
where the time goes in v4:
time: 59.7 us; the launch traced here: 59.1 us
  waiting for transfers between devices  40.4 us (68%)
  starting transfers between devices  12.3 us (21%)
  Pallas kernels  4.57 us (8%)
  local copies, waits for them, and re-layouts  1.7 us (3%)
    ppermute x4, waiting for transfers between devices, send(): return lax.ppermute(value, axes, pairs)  37.6 us
    ppermute x4, starting transfers between devices, shifted(): return lax.ppermute(value, axes, pairs_of(axis, step, groups))  8.43 us
    pallas_call x5, Pallas kernels, placed(): run(*(a if s is ANY_SPEC else pltpu.with_memory_space_constraint(a, s.mem...  4.57 us
    ppermute x4, starting transfers between devices, send(): return lax.ppermute(value, axes, pairs)  3.91 us
    ppermute x4, waiting for transfers between devices, shifted(): return lax.ppermute(value, axes, pairs_of(axis, step, groups))  2.72 us
    cond x4, local copies, waits for them, and re-layouts  1.69 us
  transfers between devices with their start and end apart: 8, of which 4 were waited for; matrix products, arithmetic and copies ran while one was open for 0% of the time, Pallas kernels for 5%

profile of v4, /device:TPU:58, one launch (start us, length us, event | category | flops | bytes accessed | tf_op | source)
XLA Modules:
  0.0 59.1 jit_solution(11850889614238760921)
XLA Ops:
  0.0 10.7 %conditional.1 = (f32[280,128]{1,0:T(8,128)S(1)}, f32[280,128]{1,0:T(8,128)S(1)}, f32[96,128]{1,0:T(8,128)S(1)}, f32[96,128]{1,0:T(8,128)S(1)}, f32[24,128]{1,0:...) conditional(s32[]{:T(128)} %convert_element_type.3, (f32[512,128]{1,0:T(8,128)}, ...), branch_computations={%region_0.0_spmd, %region_1.0_spmd} | conditional | bytes 3211488 | solution.py:473
  0.0 0.0 copy-start
  0.0 0.9 %copy-done = f32[512,128]{1,0:T(8,128)S(1)} copy-done((f32[512,128]{1,0:T(8,128)S(1)}, f32[512,128]{1,0:T(8,128)}, u32[]{:S(2)}) %copy-start) | copy-done | bytes 262168 | tf_op jit(solution)/shard_map/cond
  1.0 0.0 copy-start.2
  1.0 0.7 %copy-done.2 = f32[48,128]{1,0:T(8,128)S(1)} copy-done((f32[48,128]{1,0:T(8,128)S(1)}, f32[48,128]{1,0:T(8,128)}, u32[]{:S(2)}) %copy-start.2) | copy-done | bytes 24600 | tf_op jit(solution)/shard_map/cond
  1.7 1.3 %collective-permute-start = (f32[280,128]{1,0:T(8,128)S(1)}, f32[280,128]{1,0:T(8,128)S(1)}, u32[]{:S(2)}, u32[]{:S(2)}) collective-permute-start(f32[280,128]{1,0:T(8,128)S(1)} %get-tuple-element.17), channel_id=1, source_target_pairs={{0,8},{1,9},{2,10},{3,11},{4,12},{5,13},{6,14},{7,15},{8,16},{9,17... | collective-permute-start | bytes 430088 | tf_op jit(solution)/shard_map/cond/branch_0_fun/ppermute | solution.py:426
  3.0 4.6 %collective-permute-start.1 = (f32[280,128]{1,0:T(8,128)S(1)}, f32[280,128]{1,0:T(8,128)S(1)}, u32[]{:S(2)}, u32[]{:S(2)}) collective-permute-start(f32[280,128]{1,0:T(8,128)S(1)} %get-tuple-element.18), channel_id=1, source_target_pairs={{8,0},{9,1},{10,2},{11,3},{12,4},{13,5},{14,6},{15,7},{16,8},{17,9... | collective-permute-start | bytes 430088 | tf_op jit(solution)/shard_map/cond/branch_0_fun/ppermute | solution.py:426
  7.6 1.5 %collective-permute-done.from_up = f32[280,128]{1,0:T(8,128)S(1)} collective-permute-done((f32[280,128]{1,0:T(8,128)S(1)}, f32[280,128]{1,0:T(8,128)S(1)}, u32[]{:S(2)}, u32[]{:S(2)}) %collective-permute-start) | collective-permute-done | bytes 143392 | tf_op jit(solution)/shard_map/cond/branch_0_fun/ppermute | solution.py:426
  9.1 1.2 %collective-permute-done.1.from_down = f32[280,128]{1,0:T(8,128)S(1)} collective-permute-done((f32[280,128]{1,0:T(8,128)S(1)}, f32[280,128]{1,0:T(8,128)S(1)}, u32[]{:S(2)}, u32[]{:S(2)}) %collective-permute-start.1) | collective-permute-done | bytes 143392 | tf_op jit(solution)/shard_map/cond/branch_0_fun/ppermute | solution.py:426
  10.3 0.3 branch_0_fun.3
  10.7 1.3 %collective-permute-start.4 = (f32[96,128]{1,0:T(8,128)S(1)}, f32[96,128]{1,0:T(8,128)S(1)}, u32[]{:S(2)}, u32[]{:S(2)}) collective-permute-start(f32[96,128]{1,0:T(8,128)S(1)} %get-tuple-element.50), channel_id=1, source_target_pairs={{0,1},{1,2},{2,3},{3,4},{4,5},{5,6},{6,7},{8,9},{9,10},{10,11},{11... | collective-permute-start | bytes 147464 | tf_op jit(solution)/shard_map/ppermute | solution.py:426
  12.0 1.3 %collective-permute-start.5 = (f32[96,128]{1,0:T(8,128)S(1)}, f32[96,128]{1,0:T(8,128)S(1)}, u32[]{:S(2)}, u32[]{:S(2)}) collective-permute-start(f32[96,128]{1,0:T(8,128)S(1)} %get-tuple-element.51), channel_id=1, source_target_pairs={{1,0},{2,1},{3,2},{4,3},{5,4},{6,5},{7,6},{9,8},{10,9},{11,10},{12... | collective-permute-start | bytes 147464 | tf_op jit(solution)/shard_map/ppermute | solution.py:426
  13.3 0.7 %collective-permute-start.6 = (f32[24,128]{1,0:T(8,128)S(1)}, f32[24,128]{1,0:T(8,128)S(1)}, u32[]{:S(2)}, u32[]{:S(2)}) collective-permute-start(f32[24,128]{1,0:T(8,128)S(1)} %get-tuple-element.52), channel_id=1, source_target_pairs={{455,6},{463,4},{471,2},{479,0},{487,1},{495,3},{503,5},{511,7},{4... | collective-permute-start | bytes 36872 | tf_op jit(solution)/shard_map/ppermute | solution.py:483
  13.9 1.3 %collective-permute-start.7 = (f32[24,128]{1,0:T(8,128)S(1)}, f32[24,128]{1,0:T(8,128)S(1)}, u32[]{:S(2)}, u32[]{:S(2)}) collective-permute-start(f32[24,128]{1,0:T(8,128)S(1)} %get-tuple-element.53), channel_id=1, source_target_pairs={{455,62},{463,60},{471,58},{479,56},{487,57},{495,59},{503,61},{51... | collective-permute-start | bytes 36872 | tf_op jit(solution)/shard_map/ppermute | solution.py:483
  15.2 1.3 %collective-permute-start.8 = (f32[8,128]{1,0:T(8,128)S(1)}, f32[8,128]{1,0:T(8,128)S(1)}, u32[]{:S(2)}, u32[]{:S(2)}) collective-permute-start(f32[8,128]{1,0:T(8,128)S(1)} %get-tuple-element.54), channel_id=1, source_target_pairs={{455,0},{463,8},{471,16},{479,24},{487,32},{495,40},{503,48},{511,... | collective-permute-start | bytes 12296 | tf_op jit(solution)/shard_map/ppermute | solution.py:483
  16.5 0.0 collective-permute-done.4.from_left
  16.6 0.7 %collective-permute-start.9 = (f32[8,128]{1,0:T(8,128)S(1)}, f32[8,128]{1,0:T(8,128)S(1)}, u32[]{:S(2)}, u32[]{:S(2)}) collective-permute-start(f32[8,128]{1,0:T(8,128)S(1)} %get-tuple-element.54), channel_id=1, source_target_pairs={{455,7},{463,15},{471,23},{479,31},{487,39},{495,47},{503,55},{511... | collective-permute-start | bytes 12296 | tf_op jit(solution)/shard_map/ppermute | solution.py:483
  17.2 1.0 %shard_map.46 = (f32[512,128]{1,0:T(8,128)S(1)}, f32[48,128]{1,0:T(8,128)S(1)}) custom-call(f32[512,128]{1,0:T(8,128)} %bitcast.10, f32[48,128]{1,0:T(8,128)} %bitcast.14), custom_call_target="tpu_custom_call" | custom-call | tf_op jit(solution)/shard_map/pallas_call | solution.py:399
  18.2 0.0 collective-permute-done.5.from_right
  18.2 0.0 copy-start.4
  18.2 2.0 %shard_map.47.moved = f32[512,128]{1,0:T(8,128)S(1)} custom-call(f32[512,128]{1,0:T(8,128)S(1)} %get-tuple-element.46.state, f32[48,128]{1,0:T(8,128)S(1)} %get-tuple-element.47.metric, f32[280,128]{1,0:T(8,128)S(1)} %get-tuple-element.48.from_up, f32[280,128]{1,0:T(8,128)S(1)} %get-tuple-element.49.from_down, ...), custom_call_target="tpu_custom_call" | custom-call | tf_op jit(solution)/shard_map/pallas_call | solution.py:399
  20.2 31.8 %collective-permute-done.8.south = f32[8,128]{1,0:T(8,128)S(1)} collective-permute-done((f32[8,128]{1,0:T(8,128)S(1)}, f32[8,128]{1,0:T(8,128)S(1)}, u32[]{:S(2)}, u32[]{:S(2)}) %collective-permute-start.8) | collective-permute-done | bytes 4128 | tf_op jit(solution)/shard_map/ppermute | solution.py:483
  52.1 0.0 collective-permute-done.9.north
  52.1 0.0 collective-permute-done.6.west
  52.1 5.8 %collective-permute-done.7.east = f32[24,128]{1,0:T(8,128)S(1)} collective-permute-done((f32[24,128]{1,0:T(8,128)S(1)}, f32[24,128]{1,0:T(8,128)S(1)}, u32[]{:S(2)}, u32[]{:S(2)}) %collective-permute-start.7) | collective-permute-done | bytes 12320 | tf_op jit(solution)/shard_map/ppermute | solution.py:483
  57.9 0.0 copy-done.4
  57.9 1.2 %shard_map.48 = f32[512,128]{1,0:T(8,128)} custom-call(f32[512,128]{1,0:T(8,128)S(1)} %shard_map.47.moved, f32[24,128]{1,0:T(8,128)S(1)} %collective-permute-done.6.west, f32[24,128]{1,0:T(8,128)S(1)} %collective-permute-done.7.east, f32[8,128]{1,0:T(8,128)S(1)} %collective-permute-done.8.south, f32[8,128]{1,0:T(8,128)S(1)} %collective-permute-done.9.north, ...), custom_call_target="tpu_custom_call" | custom-call | tf_op jit(solution)/shard_map/pallas_call | solution.py:399
  (4 shorter events, 0.0 us)
Async XLA Ops:
  0.0 0.9 %copy-start = (f32[512,128]{1,0:T(8,128)S(1)}, f32[512,128]{1,0:T(8,128)}, u32[]{:S(2)}) copy-start(f32[512,128]{1,0:T(8,128)} %get-tuple-element.15.state) | copy-start | bytes 786436 | tf_op jit(solution)/shard_map/cond
  1.0 0.7 %copy-start.2 = (f32[48,128]{1,0:T(8,128)S(1)}, f32[48,128]{1,0:T(8,128)}, u32[]{:S(2)}) copy-start(f32[48,128]{1,0:T(8,128)} %get-tuple-element.16.metric) | copy-start | bytes 73732 | tf_op jit(solution)/shard_map/cond
  1.7 7.4 %collective-permute-start = (f32[280,128]{1,0:T(8,128)S(1)}, f32[280,128]{1,0:T(8,128)S(1)}, u32[]{:S(2)}, u32[]{:S(2)}) collective-permute-start(f32[280,128]{1,0:T(8,128)S(1)} %get-tuple-element.17), channel_id=1, source_target_pairs={{0,8},{1,9},{2,10},{3,11},{4,12},{5,13},{6,14},{7,15},{8,16},{9,17... | collective-permute-start | bytes 430088 | tf_op jit(solution)/shard_map/cond/branch_0_fun/ppermute | solution.py:426
  3.0 7.3 %collective-permute-start.1 = (f32[280,128]{1,0:T(8,128)S(1)}, f32[280,128]{1,0:T(8,128)S(1)}, u32[]{:S(2)}, u32[]{:S(2)}) collective-permute-start(f32[280,128]{1,0:T(8,128)S(1)} %get-tuple-element.18), channel_id=1, source_target_pairs={{8,0},{9,1},{10,2},{11,3},{12,4},{13,5},{14,6},{15,7},{16,8},{17,9... | collective-permute-start | bytes 430088 | tf_op jit(solution)/shard_map/cond/branch_0_fun/ppermute | solution.py:426
  10.7 5.9 %collective-permute-start.4 = (f32[96,128]{1,0:T(8,128)S(1)}, f32[96,128]{1,0:T(8,128)S(1)}, u32[]{:S(2)}, u32[]{:S(2)}) collective-permute-start(f32[96,128]{1,0:T(8,128)S(1)} %get-tuple-element.50), channel_id=1, source_target_pairs={{0,1},{1,2},{2,3},{3,4},{4,5},{5,6},{6,7},{8,9},{9,10},{10,11},{11... | collective-permute-start | bytes 147464 | tf_op jit(solution)/shard_map/ppermute | solution.py:426
  12.0 6.2 %collective-permute-start.5 = (f32[96,128]{1,0:T(8,128)S(1)}, f32[96,128]{1,0:T(8,128)S(1)}, u32[]{:S(2)}, u32[]{:S(2)}) collective-permute-start(f32[96,128]{1,0:T(8,128)S(1)} %get-tuple-element.51), channel_id=1, source_target_pairs={{1,0},{2,1},{3,2},{4,3},{5,4},{6,5},{7,6},{9,8},{10,9},{11,10},{12... | collective-permute-start | bytes 147464 | tf_op jit(solution)/shard_map/ppermute | solution.py:426
  13.3 38.8 %collective-permute-start.6 = (f32[24,128]{1,0:T(8,128)S(1)}, f32[24,128]{1,0:T(8,128)S(1)}, u32[]{:S(2)}, u32[]{:S(2)}) collective-permute-start(f32[24,128]{1,0:T(8,128)S(1)} %get-tuple-element.52), channel_id=1, source_target_pairs={{455,6},{463,4},{471,2},{479,0},{487,1},{495,3},{503,5},{511,7},{4... | collective-permute-start | bytes 36872 | tf_op jit(solution)/shard_map/ppermute | solution.py:483
  13.9 43.9 %collective-permute-start.7 = (f32[24,128]{1,0:T(8,128)S(1)}, f32[24,128]{1,0:T(8,128)S(1)}, u32[]{:S(2)}, u32[]{:S(2)}) collective-permute-start(f32[24,128]{1,0:T(8,128)S(1)} %get-tuple-element.53), channel_id=1, source_target_pairs={{455,62},{463,60},{471,58},{479,56},{487,57},{495,59},{503,61},{51... | collective-permute-start | bytes 36872 | tf_op jit(solution)/shard_map/ppermute | solution.py:483
  15.2 36.8 %collective-permute-start.8 = (f32[8,128]{1,0:T(8,128)S(1)}, f32[8,128]{1,0:T(8,128)S(1)}, u32[]{:S(2)}, u32[]{:S(2)}) collective-permute-start(f32[8,128]{1,0:T(8,128)S(1)} %get-tuple-element.54), channel_id=1, source_target_pairs={{455,0},{463,8},{471,16},{479,24},{487,32},{495,40},{503,48},{511,... | collective-permute-start | bytes 12296 | tf_op jit(solution)/shard_map/ppermute | solution.py:483
  16.6 35.5 %collective-permute-start.9 = (f32[8,128]{1,0:T(8,128)S(1)}, f32[8,128]{1,0:T(8,128)S(1)}, u32[]{:S(2)}, u32[]{:S(2)}) collective-permute-start(f32[8,128]{1,0:T(8,128)S(1)} %get-tuple-element.54), channel_id=1, source_target_pairs={{455,7},{463,15},{471,23},{479,31},{487,39},{495,47},{503,55},{511... | collective-permute-start | bytes 12296 | tf_op jit(solution)/shard_map/ppermute | solution.py:483
  18.2 39.7 %copy-start.4 = (s32[7,4]{0,1:T(4,128)S(1)}, s32[7,4]{0,1:T(4,128)}, u32[]{:S(2)}) copy-start(s32[7,4]{0,1:T(4,128)} %param.9) | copy-start | bytes 340

commit v5 on v4

--- a/solution.py
+++ b/solution.py
@@ -133,7 +133,8 @@
     return plane_row(state, metric, plane, (rt - 1) * 8, 8)
 
 
-def pack_kernel(state, metric, from_up, from_down, left, right, above, below):
+def pack_kernel(state, metric, from_up, from_down, far, near, above, below):
+    odd = lax.axis_index("gy") % 2 == 1
     above[...] = from_up[...]
     below[...] = from_down[...]
     lane = iota((8, LANES), 1) // 8
@@ -150,8 +151,8 @@
                 shift = (8 * s + 8) % LANES
                 right_sum = jnp.where(lane == s, pltpu.roll(value, shift, 1) if shift else value, right_sum)
             at = (rt * 3 + group) * 8
-            left[at : at + 8, :] = left_sum
-            right[at : at + 8, :] = right_sum
+            far[at : at + 8, :] = jnp.where(odd, right_sum, left_sum)
+            near[at : at + 8, :] = jnp.where(odd, left_sum, right_sum)
 
 
 def next_col(centre, halo, lane):
@@ -170,24 +171,28 @@
 EXT = ROWS + 2 * HALO
 
 
-def advance_kernel(state, metric, from_up, from_down, from_left, from_right, out, wide, terrain):
+def advance_kernel(state, metric, from_up, from_down, from_far, from_near, out, wide, terrain):
     gx = lax.axis_index("gx")
     gy = lax.axis_index("gy")
+    odd = gy % 2 == 1
     lane8 = iota((8, LANES), 1)
-    for plane in range(PLANES):
-        group, s = divmod(plane, 16)
-        for rt in range(4):
+    for rt in range(4):
+        for group in range(3):
             at = (rt * 3 + group) * 8
-            right_part = pltpu.roll(from_right[at : at + 8, :], (LANES - 8 * s) % LANES, 1)
-            left_part = pltpu.roll(from_left[at : at + 8, :], (120 - 8 * s) % LANES, 1)
-            halo = jnp.where(lane8 < 8, right_part, jnp.where(lane8 >= 120, left_part, 0.0))
-            centre = strip(state, metric, from_up, from_down, plane, rt)
-            if plane < 4 * L:
-                wide[plane, 0, rt * 8 : rt * 8 + 8, :] = centre
-                wide[plane, 1, rt * 8 : rt * 8 + 8, :] = halo
-            else:
-                terrain[plane - 4 * L, 0, rt * 8 : rt * 8 + 8, :] = centre
-                terrain[plane - 4 * L, 1, rt * 8 : rt * 8 + 8, :] = halo
+            far, near = from_far[at : at + 8, :], from_near[at : at + 8, :]
+            from_left, from_right = jnp.where(odd, near, far), jnp.where(odd, far, near)
+            for s in range(min(16, PLANES - group * 16)):
+                plane = group * 16 + s
+                right_part = pltpu.roll(from_right, (LANES - 8 * s) % LANES, 1)
+                left_part = pltpu.roll(from_left, (120 - 8 * s) % LANES, 1)
+                halo = jnp.where(lane8 < 8, right_part, jnp.where(lane8 >= 120, left_part, 0.0))
+                centre = strip(state, metric, from_up, from_down, plane, rt)
+                if plane < 4 * L:
+                    wide[plane, 0, rt * 8 : rt * 8 + 8, :] = centre
+                    wide[plane, 1, rt * 8 : rt * 8 + 8, :] = halo
+                else:
+                    terrain[plane - 4 * L, 0, rt * 8 : rt * 8 + 8, :] = centre
+                    terrain[plane - 4 * L, 1, rt * 8 : rt * 8 + 8, :] = halo
 
     row = iota((EXT, LANES), 0) + ROWS * gx - HALO
     lane = iota((EXT, LANES), 1)
@@ -459,18 +464,18 @@
             near=False,
         )(first, info)
         arrived = lax.all_to_all(second.reshape(8, FINE, LANES), "gx", 0, 0).reshape(8 * FINE, LANES)
-        left, right, above, below = packed(flat, ground, from_up, from_down)
+        far, near, above, below = packed(flat, ground, from_up, from_down)
         parts = call(merge_kernel, (V, V), [(THREE, LANES), (THREE, LANES), (8, LANES)])(arrived, info)
-        return (above, below, left, right, *parts)
+        return (above, below, far, near, *parts)
 
     def as_nest(flat, ground, placement):
         others = range(NESTS)
         from_up, from_down = rows_halo(flat, ground, others)
-        left, right, above, below = packed(flat, ground, from_up, from_down)
+        far, near, above, below = packed(flat, ground, from_up, from_down)
         none = jnp.zeros((THREE, LANES), F32)
-        return above, below, left, right, none, none, none[:8]
-
-    from_up, from_down, left, right, across, beyond, along = lax.cond(
+        return above, below, far, near, none, none, none[:8]
+
+    from_up, from_down, far, near, across, beyond, along = lax.cond(
         lax.axis_index("nest") == NESTS, as_parent, as_nest, flat, ground, placement
     )
 
@@ -486,15 +491,25 @@
     east = send(beyond, lambda g, q: (7, q))
     top = send(along, lambda g, q: (g, 7))
     bottom = send(along, lambda g, q: (g, 0))
-    everyone = range(NESTS + 1)
-    from_left, from_right = shifted(right, 1, 1, everyone), shifted(left, 1, -1, everyone)
+
+    def swapped(value, first):
+        pairs = []
+        for n in range(NESTS + 1):
+            for x in range(8):
+                for y in range(first, 7, 2):
+                    a = (n * 8 + x) * 8 + y
+                    pairs += [(a, a + 1), (a + 1, a)]
+        return lax.ppermute(value, axes, pairs)
+
+    from_far = swapped(far, 1)
+    from_near = swapped(near, 0)
     flat, ground = call(fetch_kernel, (A, A), [(4 * L * ROWS, LANES), (3 * ROWS, LANES)], [DMA((2,))])(flat, ground)
     (moved,) = call(
         advance_kernel,
         (V,) * 6,
         [(4 * L * ROWS, LANES)],
         [pltpu.VMEM((4 * L, 2, EXT, LANES), F32), pltpu.VMEM((4, 2, EXT, LANES), F32)],
-    )(flat, ground, from_up, from_down, from_left, from_right)
+    )(flat, ground, from_up, from_down, from_far, from_near)
     (result,) = call(
         relax_kernel,
         (V,) * 6,

time: 59.7 us -> 59.7 us (level)
  starting transfers between devices: 12.3 us -> 16.1 us
  waiting for transfers between devices: 40.4 us -> 36.6 us
    ppermute x0 -> x2, starting transfers between devices: none -> 6.3 us  [swapped(): return lax.ppermute(value, axes, pairs)]
    ppermute x4, waiting for transfers between devices: 37.6 us -> 33.9 us  [send(): return lax.ppermute(value, axes, pairs)]
    ppermute x4 -> x2, starting transfers between devices: 8.43 us -> 5.85 us  [shifted(): return lax.ppermute(value, axes, pairs_of(axis, step, groups))]
    ppermute x4 -> x2, waiting for transfers between devices: 2.72 us -> 2.71 us  [shifted(): return lax.ppermute(value, axes, pairs_of(axis, step, groups))]
where the time goes in v5:
time: 59.7 us; the launch traced here: 59.1 us
  waiting for transfers between devices  36.6 us (61%)
  starting transfers between devices  16.1 us (27%)
  Pallas kernels  4.58 us (8%)
  local copies, waits for them, and re-layouts  1.7 us (3%)
    ppermute x4, waiting for transfers between devices, send(): return lax.ppermute(value, axes, pairs)  33.9 us
    ppermute x2, starting transfers between devices, swapped(): return lax.ppermute(value, axes, pairs)  6.3 us
    ppermute x2, starting transfers between devices, shifted(): return lax.ppermute(value, axes, pairs_of(axis, step, groups))  5.85 us
    pallas_call x5, Pallas kernels, placed(): run(*(a if s is ANY_SPEC else pltpu.with_memory_space_constraint(a, s.mem...  4.58 us
    ppermute x4, starting transfers between devices, send(): return lax.ppermute(value, axes, pairs)  3.91 us
    ppermute x2, waiting for transfers between devices, shifted(): return lax.ppermute(value, axes, pairs_of(axis, step, groups))  2.71 us
    cond x4, local copies, waits for them, and re-layouts  1.69 us
  transfers between devices with their start and end apart: 8, of which 4 were waited for; matrix products, arithmetic and copies ran while one was open for 0% of the time, Pallas kernels for 5%

profile of v5, /device:TPU:58, one launch (start us, length us, event | category | flops | bytes accessed | tf_op | source)
XLA Modules:
  0.0 59.1 jit_solution(10368353764118814133)
XLA Ops:
  0.0 10.7 %conditional.1 = (f32[280,128]{1,0:T(8,128)S(1)}, f32[280,128]{1,0:T(8,128)S(1)}, f32[96,128]{1,0:T(8,128)S(1)}, f32[96,128]{1,0:T(8,128)S(1)}, f32[24,128]{1,0:...) conditional(s32[]{:T(128)} %convert_element_type.3, (f32[512,128]{1,0:T(8,128)}, ...), branch_computations={%region_0.0_spmd, %region_1.0_spmd} | conditional | bytes 3211488 | solution.py:478
  0.0 0.0 copy-start
  0.0 0.9 %copy-done = f32[512,128]{1,0:T(8,128)S(1)} copy-done((f32[512,128]{1,0:T(8,128)S(1)}, f32[512,128]{1,0:T(8,128)}, u32[]{:S(2)}) %copy-start) | copy-done | bytes 262168 | tf_op jit(solution)/shard_map/cond
  1.0 0.0 copy-start.2
  1.0 0.7 %copy-done.2 = f32[48,128]{1,0:T(8,128)S(1)} copy-done((f32[48,128]{1,0:T(8,128)S(1)}, f32[48,128]{1,0:T(8,128)}, u32[]{:S(2)}) %copy-start.2) | copy-done | bytes 24600 | tf_op jit(solution)/shard_map/cond
  1.7 1.3 %collective-permute-start = (f32[280,128]{1,0:T(8,128)S(1)}, f32[280,128]{1,0:T(8,128)S(1)}, u32[]{:S(2)}, u32[]{:S(2)}) collective-permute-start(f32[280,128]{1,0:T(8,128)S(1)} %get-tuple-element.17), channel_id=1, source_target_pairs={{0,8},{1,9},{2,10},{3,11},{4,12},{5,13},{6,14},{7,15},{8,16},{9,17... | collective-permute-start | bytes 430088 | tf_op jit(solution)/shard_map/cond/branch_0_fun/ppermute | solution.py:431
  3.0 4.6 %collective-permute-start.1 = (f32[280,128]{1,0:T(8,128)S(1)}, f32[280,128]{1,0:T(8,128)S(1)}, u32[]{:S(2)}, u32[]{:S(2)}) collective-permute-start(f32[280,128]{1,0:T(8,128)S(1)} %get-tuple-element.18), channel_id=1, source_target_pairs={{8,0},{9,1},{10,2},{11,3},{12,4},{13,5},{14,6},{15,7},{16,8},{17,9... | collective-permute-start | bytes 430088 | tf_op jit(solution)/shard_map/cond/branch_0_fun/ppermute | solution.py:431
  7.6 1.5 %collective-permute-done.from_up = f32[280,128]{1,0:T(8,128)S(1)} collective-permute-done((f32[280,128]{1,0:T(8,128)S(1)}, f32[280,128]{1,0:T(8,128)S(1)}, u32[]{:S(2)}, u32[]{:S(2)}) %collective-permute-start) | collective-permute-done | bytes 143392 | tf_op jit(solution)/shard_map/cond/branch_0_fun/ppermute | solution.py:431
  9.1 1.2 %collective-permute-done.1.from_down = f32[280,128]{1,0:T(8,128)S(1)} collective-permute-done((f32[280,128]{1,0:T(8,128)S(1)}, f32[280,128]{1,0:T(8,128)S(1)}, u32[]{:S(2)}, u32[]{:S(2)}) %collective-permute-start.1) | collective-permute-done | bytes 143392 | tf_op jit(solution)/shard_map/cond/branch_0_fun/ppermute | solution.py:431
  10.3 0.3 branch_0_fun.3
  10.7 0.7 %collective-permute-start.4 = (f32[96,128]{1,0:T(8,128)S(1)}, f32[96,128]{1,0:T(8,128)S(1)}, u32[]{:S(2)}, u32[]{:S(2)}) collective-permute-start(f32[96,128]{1,0:T(8,128)S(1)} %get-tuple-element.50), channel_id=1, source_target_pairs={{1,2},{2,1},{3,4},{4,3},{5,6},{6,5},{9,10},{10,9},{11,12},{12,11},... | collective-permute-start | bytes 147464 | tf_op jit(solution)/shard_map/ppermute | solution.py:502
  11.3 5.6 %collective-permute-start.5 = (f32[96,128]{1,0:T(8,128)S(1)}, f32[96,128]{1,0:T(8,128)S(1)}, u32[]{:S(2)}, u32[]{:S(2)}) collective-permute-start(f32[96,128]{1,0:T(8,128)S(1)} %get-tuple-element.51), channel_id=1, source_target_pairs={{0,1},{1,0},{2,3},{3,2},{4,5},{5,4},{6,7},{7,6},{8,9},{9,8},{10,11... | collective-permute-start | bytes 147464 | tf_op jit(solution)/shard_map/ppermute | solution.py:502
  17.0 0.7 %collective-permute-start.6 = (f32[24,128]{1,0:T(8,128)S(1)}, f32[24,128]{1,0:T(8,128)S(1)}, u32[]{:S(2)}, u32[]{:S(2)}) collective-permute-start(f32[24,128]{1,0:T(8,128)S(1)} %get-tuple-element.52), channel_id=1, source_target_pairs={{455,6},{463,4},{471,2},{479,0},{487,1},{495,3},{503,5},{511,7},{4... | collective-permute-start | bytes 36872 | tf_op jit(solution)/shard_map/ppermute | solution.py:488
  17.7 1.3 %collective-permute-start.7 = (f32[24,128]{1,0:T(8,128)S(1)}, f32[24,128]{1,0:T(8,128)S(1)}, u32[]{:S(2)}, u32[]{:S(2)}) collective-permute-start(f32[24,128]{1,0:T(8,128)S(1)} %get-tuple-element.53), channel_id=1, source_target_pairs={{455,62},{463,60},{471,58},{479,56},{487,57},{495,59},{503,61},{51... | collective-permute-start | bytes 36872 | tf_op jit(solution)/shard_map/ppermute | solution.py:488
  19.0 1.3 %collective-permute-start.8 = (f32[8,128]{1,0:T(8,128)S(1)}, f32[8,128]{1,0:T(8,128)S(1)}, u32[]{:S(2)}, u32[]{:S(2)}) collective-permute-start(f32[8,128]{1,0:T(8,128)S(1)} %get-tuple-element.54), channel_id=1, source_target_pairs={{455,0},{463,8},{471,16},{479,24},{487,32},{495,40},{503,48},{511,... | collective-permute-start | bytes 12296 | tf_op jit(solution)/shard_map/ppermute | solution.py:488
  20.3 0.0 collective-permute-done.4.from_far
  20.3 0.7 %collective-permute-start.9 = (f32[8,128]{1,0:T(8,128)S(1)}, f32[8,128]{1,0:T(8,128)S(1)}, u32[]{:S(2)}, u32[]{:S(2)}) collective-permute-start(f32[8,128]{1,0:T(8,128)S(1)} %get-tuple-element.54), channel_id=1, source_target_pairs={{455,7},{463,15},{471,23},{479,31},{487,39},{495,47},{503,55},{511... | collective-permute-start | bytes 12296 | tf_op jit(solution)/shard_map/ppermute | solution.py:488
  20.9 1.0 %shard_map.46 = (f32[512,128]{1,0:T(8,128)S(1)}, f32[48,128]{1,0:T(8,128)S(1)}) custom-call(f32[512,128]{1,0:T(8,128)} %bitcast.10, f32[48,128]{1,0:T(8,128)} %bitcast.14), custom_call_target="tpu_custom_call" | custom-call | tf_op jit(solution)/shard_map/pallas_call | solution.py:404
  21.9 0.0 collective-permute-done.5.from_near
  21.9 0.0 copy-start.4
  21.9 2.0 %shard_map.47.moved = f32[512,128]{1,0:T(8,128)S(1)} custom-call(f32[512,128]{1,0:T(8,128)S(1)} %get-tuple-element.46.state, f32[48,128]{1,0:T(8,128)S(1)} %get-tuple-element.47.metric, f32[280,128]{1,0:T(8,128)S(1)} %get-tuple-element.48.from_up, f32[280,128]{1,0:T(8,128)S(1)} %get-tuple-element.49.from_down, ...), custom_call_target="tpu_custom_call" | custom-call | tf_op jit(solution)/shard_map/pallas_call | solution.py:404
  24.0 28.1 %collective-permute-done.8.south = f32[8,128]{1,0:T(8,128)S(1)} collective-permute-done((f32[8,128]{1,0:T(8,128)S(1)}, f32[8,128]{1,0:T(8,128)S(1)}, u32[]{:S(2)}, u32[]{:S(2)}) %collective-permute-start.8) | collective-permute-done | bytes 4128 | tf_op jit(solution)/shard_map/ppermute | solution.py:488
  52.1 0.0 collective-permute-done.9.north
  52.1 0.0 collective-permute-done.6.west
  52.1 5.8 %collective-permute-done.7.east = f32[24,128]{1,0:T(8,128)S(1)} collective-permute-done((f32[24,128]{1,0:T(8,128)S(1)}, f32[24,128]{1,0:T(8,128)S(1)}, u32[]{:S(2)}, u32[]{:S(2)}) %collective-permute-start.7) | collective-permute-done | bytes 12320 | tf_op jit(solution)/shard_map/ppermute | solution.py:488
  57.9 0.0 copy-done.4
  57.9 1.2 %shard_map.48 = f32[512,128]{1,0:T(8,128)} custom-call(f32[512,128]{1,0:T(8,128)S(1)} %shard_map.47.moved, f32[24,128]{1,0:T(8,128)S(1)} %collective-permute-done.6.west, f32[24,128]{1,0:T(8,128)S(1)} %collective-permute-done.7.east, f32[8,128]{1,0:T(8,128)S(1)} %collective-permute-done.8.south, f32[8,128]{1,0:T(8,128)S(1)} %collective-permute-done.9.north, ...), custom_call_target="tpu_custom_call" | custom-call | tf_op jit(solution)/shard_map/pallas_call | solution.py:404
  (4 shorter events, 0.0 us)
Async XLA Ops:
  0.0 0.9 %copy-start = (f32[512,128]{1,0:T(8,128)S(1)}, f32[512,128]{1,0:T(8,128)}, u32[]{:S(2)}) copy-start(f32[512,128]{1,0:T(8,128)} %get-tuple-element.15.state) | copy-start | bytes 786436 | tf_op jit(solution)/shard_map/cond
  1.0 0.7 %copy-start.2 = (f32[48,128]{1,0:T(8,128)S(1)}, f32[48,128]{1,0:T(8,128)}, u32[]{:S(2)}) copy-start(f32[48,128]{1,0:T(8,128)} %get-tuple-element.16.metric) | copy-start | bytes 73732 | tf_op jit(solution)/shard_map/cond
  1.7 7.4 %collective-permute-start = (f32[280,128]{1,0:T(8,128)S(1)}, f32[280,128]{1,0:T(8,128)S(1)}, u32[]{:S(2)}, u32[]{:S(2)}) collective-permute-start(f32[280,128]{1,0:T(8,128)S(1)} %get-tuple-element.17), channel_id=1, source_target_pairs={{0,8},{1,9},{2,10},{3,11},{4,12},{5,13},{6,14},{7,15},{8,16},{9,17... | collective-permute-start | bytes 430088 | tf_op jit(solution)/shard_map/cond/branch_0_fun/ppermute | solution.py:431
  3.0 7.3 %collective-permute-start.1 = (f32[280,128]{1,0:T(8,128)S(1)}, f32[280,128]{1,0:T(8,128)S(1)}, u32[]{:S(2)}, u32[]{:S(2)}) collective-permute-start(f32[280,128]{1,0:T(8,128)S(1)} %get-tuple-element.18), channel_id=1, source_target_pairs={{8,0},{9,1},{10,2},{11,3},{12,4},{13,5},{14,6},{15,7},{16,8},{17,9... | collective-permute-start | bytes 430088 | tf_op jit(solution)/shard_map/cond/branch_0_fun/ppermute | solution.py:431
  10.7 9.6 %collective-permute-start.4 = (f32[96,128]{1,0:T(8,128)S(1)}, f32[96,128]{1,0:T(8,128)S(1)}, u32[]{:S(2)}, u32[]{:S(2)}) collective-permute-start(f32[96,128]{1,0:T(8,128)S(1)} %get-tuple-element.50), channel_id=1, source_target_pairs={{1,2},{2,1},{3,4},{4,3},{5,6},{6,5},{9,10},{10,9},{11,12},{12,11},... | collective-permute-start | bytes 147464 | tf_op jit(solution)/shard_map/ppermute | solution.py:502
  11.3 10.6 %collective-permute-start.5 = (f32[96,128]{1,0:T(8,128)S(1)}, f32[96,128]{1,0:T(8,128)S(1)}, u32[]{:S(2)}, u32[]{:S(2)}) collective-permute-start(f32[96,128]{1,0:T(8,128)S(1)} %get-tuple-element.51), channel_id=1, source_target_pairs={{0,1},{1,0},{2,3},{3,2},{4,5},{5,4},{6,7},{7,6},{8,9},{9,8},{10,11... | collective-permute-start | bytes 147464 | tf_op jit(solution)/shard_map/ppermute | solution.py:502
  17.0 35.1 %collective-permute-start.6 = (f32[24,128]{1,0:T(8,128)S(1)}, f32[24,128]{1,0:T(8,128)S(1)}, u32[]{:S(2)}, u32[]{:S(2)}) collective-permute-start(f32[24,128]{1,0:T(8,128)S(1)} %get-tuple-element.52), channel_id=1, source_target_pairs={{455,6},{463,4},{471,2},{479,0},{487,1},{495,3},{503,5},{511,7},{4... | collective-permute-start | bytes 36872 | tf_op jit(solution)/shard_map/ppermute | solution.py:488
  17.7 40.2 %collective-permute-start.7 = (f32[24,128]{1,0:T(8,128)S(1)}, f32[24,128]{1,0:T(8,128)S(1)}, u32[]{:S(2)}, u32[]{:S(2)}) collective-permute-start(f32[24,128]{1,0:T(8,128)S(1)} %get-tuple-element.53), channel_id=1, source_target_pairs={{455,62},{463,60},{471,58},{479,56},{487,57},{495,59},{503,61},{51... | collective-permute-start | bytes 36872 | tf_op jit(solution)/shard_map/ppermute | solution.py:488
  19.0 33.2 %collective-permute-start.8 = (f32[8,128]{1,0:T(8,128)S(1)}, f32[8,128]{1,0:T(8,128)S(1)}, u32[]{:S(2)}, u32[]{:S(2)}) collective-permute-start(f32[8,128]{1,0:T(8,128)S(1)} %get-tuple-element.54), channel_id=1, source_target_pairs={{455,0},{463,8},{471,16},{479,24},{487,32},{495,40},{503,48},{511,... | collective-permute-start | bytes 12296 | tf_op jit(solution)/shard_map/ppermute | solution.py:488
  20.3 31.8 %collective-permute-start.9 = (f32[8,128]{1,0:T(8,128)S(1)}, f32[8,128]{1,0:T(8,128)S(1)}, u32[]{:S(2)}, u32[]{:S(2)}) collective-permute-start(f32[8,128]{1,0:T(8,128)S(1)} %get-tuple-element.54), channel_id=1, source_target_pairs={{455,7},{463,15},{471,23},{479,31},{487,39},{495,47},{503,55},{511... | collective-permute-start | bytes 12296 | tf_op jit(solution)/shard_map/ppermute | solution.py:488
  21.9 36.0 %copy-start.4 = (s32[7,4]{0,1:T(4,128)S(1)}, s32[7,4]{0,1:T(4,128)}, u32[]{:S(2)}) copy-start(s32[7,4]{0,1:T(4,128)} %param.9) | copy-start | bytes 340

commit v6 on v5

--- a/solution.py
+++ b/solution.py
@@ -39,7 +39,9 @@
 def pieces_of(n):
     far = sorted(range(8), key=lambda q: -ring(4 + SEAT[n] // 2, 4 * (n % 2) + q // 2))
     near = sorted(range(8), key=lambda g: max(ring(g, 0), ring(g, 7)))
-    return tuple(q for _, q in sorted(zip(near, far)))
+    order = [q for _, q in sorted(zip(near, far))]
+    order[3], order[4] = order[4], order[3]
+    return tuple(order)
 
 
 PIECE = tuple(pieces_of(n) for n in range(NESTS))
@@ -117,14 +119,6 @@
         down[plane * 8 : plane * 8 + 8, :] = plane_row(state, metric, plane, 8, 8)
 
 
-def fetch_kernel(state, metric, fields, ground, sems):
-    copies = [pltpu.make_async_copy(a, b, sems.at[i]) for i, (a, b) in enumerate(((state, fields), (metric, ground)))]
-    for one in copies:
-        one.start()
-    for one in copies:
-        one.wait()
-
-
 def strip(state, metric, from_up, from_down, plane, rt):
     if rt == 0:
         return from_up[plane * 8 : plane * 8 + 8, :]
@@ -133,7 +127,9 @@
     return plane_row(state, metric, plane, (rt - 1) * 8, 8)
 
 
-def pack_kernel(state, metric, from_up, from_down, far, near, above, below):
+def pack_kernel(state, metric, from_up, from_down, far, near, above, below, fields, terrain):
+    fields[...] = state[...]
+    terrain[...] = metric[...]
     odd = lax.axis_index("gy") % 2 == 1
     above[...] = from_up[...]
     below[...] = from_down[...]
@@ -434,10 +430,10 @@
         to_up, to_down = call(edge_kernel, (V, V), [(PLANES * 8, LANES)] * 2)(flat, ground)
         return shifted(to_down, 0, 1, groups), shifted(to_up, 0, -1, groups)
 
+    kept = [(96, LANES)] * 2 + [(PLANES * 8, LANES)] * 2 + [(4 * L * ROWS, LANES), (3 * ROWS, LANES)]
+
     def packed(flat, ground, from_up, from_down):
-        return call(pack_kernel, (V,) * 4, [(96, LANES)] * 2 + [(PLANES * 8, LANES)] * 2)(
-            flat, ground, from_up, from_down
-        )
+        return call(pack_kernel, (V,) * 4, kept)(flat, ground, from_up, from_down)
 
     def as_parent(flat, ground, placement):
         mine = (NESTS,)
@@ -464,18 +460,18 @@
             near=False,
         )(first, info)
         arrived = lax.all_to_all(second.reshape(8, FINE, LANES), "gx", 0, 0).reshape(8 * FINE, LANES)
-        far, near, above, below = packed(flat, ground, from_up, from_down)
+        halos = packed(flat, ground, from_up, from_down)
         parts = call(merge_kernel, (V, V), [(THREE, LANES), (THREE, LANES), (8, LANES)])(arrived, info)
-        return (above, below, far, near, *parts)
+        return (*halos, *parts)
 
     def as_nest(flat, ground, placement):
         others = range(NESTS)
         from_up, from_down = rows_halo(flat, ground, others)
-        far, near, above, below = packed(flat, ground, from_up, from_down)
+        halos = packed(flat, ground, from_up, from_down)
         none = jnp.zeros((THREE, LANES), F32)
-        return above, below, far, near, none, none, none[:8]
-
-    from_up, from_down, far, near, across, beyond, along = lax.cond(
+        return (*halos, none, none, none[:8])
+
+    far, near, from_up, from_down, flat, ground, across, beyond, along = lax.cond(
         lax.axis_index("nest") == NESTS, as_parent, as_nest, flat, ground, placement
     )
 
@@ -503,7 +499,6 @@
 
     from_far = swapped(far, 1)
     from_near = swapped(near, 0)
-    flat, ground = call(fetch_kernel, (A, A), [(4 * L * ROWS, LANES), (3 * ROWS, LANES)], [DMA((2,))])(flat, ground)
     (moved,) = call(
         advance_kernel,
         (V,) * 6,

time: 59.7 us -> 60 us (level)
  the two profiles are of different devices: /device:TPU:58 before, /device:TPU:1 now
where the time goes in v6:
time: 60 us; the launch traced here: 59 us
  waiting for transfers between devices  36.9 us (62%)
  starting transfers between devices  16.6 us (28%)
  Pallas kernels  3.61 us (6%)
  local copies, waits for them, and re-layouts  1.7 us (3%)
    ppermute x4, waiting for transfers between devices, send(): return lax.ppermute(value, axes, pairs)  32.4 us
    ppermute x2, starting transfers between devices, swapped(): return lax.ppermute(value, axes, pairs)  8.03 us
    ppermute x2, starting transfers between devices, shifted(): return lax.ppermute(value, axes, pairs_of(axis, step, groups))  5.32 us
    ppermute x2, waiting for transfers between devices, shifted(): return lax.ppermute(value, axes, pairs_of(axis, step, groups))  4.54 us
    pallas_call x4, Pallas kernels, placed(): run(*(a if s is ANY_SPEC else pltpu.with_memory_space_constraint(a, s.mem...  3.61 us
    ppermute x4, starting transfers between devices, send(): return lax.ppermute(value, axes, pairs)  3.28 us
    cond x4, local copies, waits for them, and re-layouts  1.69 us
  transfers between devices with their start and end apart: 8, of which 3 were waited for; matrix products, arithmetic and copies ran while one was open for 0% of the time, Pallas kernels for 3%

profile of v6, /device:TPU:1, one launch (start us, length us, event | category | flops | bytes accessed | tf_op | source)
XLA Modules:
  0.0 59.0 jit_solution(4618416143078204244)
XLA Ops:
  0.0 12.0 %conditional.1 = (f32[96,128]{1,0:T(8,128)S(1)}, f32[96,128]{1,0:T(8,128)S(1)}, f32[280,128]{1,0:T(8,128)S(1)}, f32[280,128]{1,0:T(8,128)S(1)}, f32[512,128]{1,0...) conditional(s32[]{:T(128)} %convert_element_type.3, ...), branch_computations={%region_0.0_spmd, %region_1.0_spmd} | conditional | bytes 3211504 | solution.py:474
  0.0 0.0 copy-start
  0.0 0.9 %copy-done = f32[512,128]{1,0:T(8,128)S(1)} copy-done((f32[512,128]{1,0:T(8,128)S(1)}, f32[512,128]{1,0:T(8,128)}, u32[]{:S(2)}) %copy-start) | copy-done | bytes 262168 | tf_op jit(solution)/shard_map/cond
  1.0 0.0 copy-start.2
  1.0 0.7 %copy-done.2 = f32[48,128]{1,0:T(8,128)S(1)} copy-done((f32[48,128]{1,0:T(8,128)S(1)}, f32[48,128]{1,0:T(8,128)}, u32[]{:S(2)}) %copy-start.2) | copy-done | bytes 24600 | tf_op jit(solution)/shard_map/cond
  1.7 4.0 %collective-permute-start = (f32[280,128]{1,0:T(8,128)S(1)}, f32[280,128]{1,0:T(8,128)S(1)}, u32[]{:S(2)}, u32[]{:S(2)}) collective-permute-start(f32[280,128]{1,0:T(8,128)S(1)} %get-tuple-element.17), channel_id=1, source_target_pairs={{0,8},{1,9},{2,10},{3,11},{4,12},{5,13},{6,14},{7,15},{8,16},{9,17... | collective-permute-start | bytes 430088 | tf_op jit(solution)/shard_map/cond/branch_0_fun/ppermute | solution.py:427
  5.7 1.3 %collective-permute-start.1 = (f32[280,128]{1,0:T(8,128)S(1)}, f32[280,128]{1,0:T(8,128)S(1)}, u32[]{:S(2)}, u32[]{:S(2)}) collective-permute-start(f32[280,128]{1,0:T(8,128)S(1)} %get-tuple-element.18), channel_id=1, source_target_pairs={{8,0},{9,1},{10,2},{11,3},{12,4},{13,5},{14,6},{15,7},{16,8},{17,9... | collective-permute-start | bytes 430088 | tf_op jit(solution)/shard_map/cond/branch_0_fun/ppermute | solution.py:427
  7.0 0.7 %collective-permute-done.from_up = f32[280,128]{1,0:T(8,128)S(1)} collective-permute-done((f32[280,128]{1,0:T(8,128)S(1)}, f32[280,128]{1,0:T(8,128)S(1)}, u32[]{:S(2)}, u32[]{:S(2)}) %collective-permute-start) | collective-permute-done | bytes 143392 | tf_op jit(solution)/shard_map/cond/branch_0_fun/ppermute | solution.py:427
  7.8 3.8 %collective-permute-done.1.from_down = f32[280,128]{1,0:T(8,128)S(1)} collective-permute-done((f32[280,128]{1,0:T(8,128)S(1)}, f32[280,128]{1,0:T(8,128)S(1)}, u32[]{:S(2)}, u32[]{:S(2)}) %collective-permute-start.1) | collective-permute-done | bytes 143392 | tf_op jit(solution)/shard_map/cond/branch_0_fun/ppermute | solution.py:427
  11.6 0.3 branch_0_fun.3
  12.0 6.1 %collective-permute-start.4 = (f32[96,128]{1,0:T(8,128)S(1)}, f32[96,128]{1,0:T(8,128)S(1)}, u32[]{:S(2)}, u32[]{:S(2)}) collective-permute-start(f32[96,128]{1,0:T(8,128)S(1)} %get-tuple-element.54), channel_id=1, source_target_pairs={{1,2},{2,1},{3,4},{4,3},{5,6},{6,5},{9,10},{10,9},{11,12},{12,11},... | collective-permute-start | bytes 147464 | tf_op jit(solution)/shard_map/ppermute | solution.py:498
  18.1 1.9 %collective-permute-start.5 = (f32[96,128]{1,0:T(8,128)S(1)}, f32[96,128]{1,0:T(8,128)S(1)}, u32[]{:S(2)}, u32[]{:S(2)}) collective-permute-start(f32[96,128]{1,0:T(8,128)S(1)} %get-tuple-element.55), channel_id=1, source_target_pairs={{0,1},{1,0},{2,3},{3,2},{4,5},{5,4},{6,7},{7,6},{8,9},{9,8},{10,11... | collective-permute-start | bytes 147464 | tf_op jit(solution)/shard_map/ppermute | solution.py:498
  20.0 1.3 %collective-permute-start.6 = (f32[24,128]{1,0:T(8,128)S(1)}, f32[24,128]{1,0:T(8,128)S(1)}, u32[]{:S(2)}, u32[]{:S(2)}) collective-permute-start(f32[24,128]{1,0:T(8,128)S(1)} %get-tuple-element.56), channel_id=1, source_target_pairs={{455,6},{463,4},{471,2},{479,1},{487,0},{495,3},{503,5},{511,7},{4... | collective-permute-start | bytes 36872 | tf_op jit(solution)/shard_map/ppermute | solution.py:484
  21.3 0.7 %collective-permute-start.7 = (f32[24,128]{1,0:T(8,128)S(1)}, f32[24,128]{1,0:T(8,128)S(1)}, u32[]{:S(2)}, u32[]{:S(2)}) collective-permute-start(f32[24,128]{1,0:T(8,128)S(1)} %get-tuple-element.57), channel_id=1, source_target_pairs={{455,62},{463,60},{471,58},{479,57},{487,56},{495,59},{503,61},{51... | collective-permute-start | bytes 36872 | tf_op jit(solution)/shard_map/ppermute | solution.py:484
  22.0 0.7 %collective-permute-start.9 = (f32[8,128]{1,0:T(8,128)S(1)}, f32[8,128]{1,0:T(8,128)S(1)}, u32[]{:S(2)}, u32[]{:S(2)}) collective-permute-start(f32[8,128]{1,0:T(8,128)S(1)} %get-tuple-element.58), channel_id=1, source_target_pairs={{455,7},{463,15},{471,23},{479,31},{487,39},{495,47},{503,55},{511... | collective-permute-start | bytes 12296 | tf_op jit(solution)/shard_map/ppermute | solution.py:484
  22.7 0.0 collective-permute-done.4.from_far
  22.7 0.7 %collective-permute-start.8 = (f32[8,128]{1,0:T(8,128)S(1)}, f32[8,128]{1,0:T(8,128)S(1)}, u32[]{:S(2)}, u32[]{:S(2)}) collective-permute-start(f32[8,128]{1,0:T(8,128)S(1)} %get-tuple-element.58), channel_id=1, source_target_pairs={{455,0},{463,8},{471,16},{479,24},{487,32},{495,40},{503,48},{511,... | collective-permute-start | bytes 12296 | tf_op jit(solution)/shard_map/ppermute | solution.py:484
  23.3 0.0 collective-permute-done.5.from_near
  23.4 0.0 copy-start.4
  23.4 2.0 %shard_map.46.moved = f32[512,128]{1,0:T(8,128)S(1)} custom-call(f32[512,128]{1,0:T(8,128)S(1)} %get-tuple-element.50.state, f32[48,128]{1,0:T(8,128)S(1)} %get-tuple-element.51.metric, f32[280,128]{1,0:T(8,128)S(1)} %get-tuple-element.52.from_up, f32[280,128]{1,0:T(8,128)S(1)} %get-tuple-element.53.from_down, ...), custom_call_target="tpu_custom_call" | custom-call | tf_op jit(solution)/shard_map/pallas_call | solution.py:400
  25.4 0.0 collective-permute-done.9.north
  25.4 0.0 collective-permute-done.8.south
  25.4 32.3 %collective-permute-done.6.west = f32[24,128]{1,0:T(8,128)S(1)} collective-permute-done((f32[24,128]{1,0:T(8,128)S(1)}, f32[24,128]{1,0:T(8,128)S(1)}, u32[]{:S(2)}, u32[]{:S(2)}) %collective-permute-start.6) | collective-permute-done | bytes 12320 | tf_op jit(solution)/shard_map/ppermute | solution.py:484
  57.8 0.0 collective-permute-done.7.east
  57.8 0.0 copy-done.4
  57.8 1.2 %shard_map.47 = f32[512,128]{1,0:T(8,128)} custom-call(f32[512,128]{1,0:T(8,128)S(1)} %shard_map.46.moved, f32[24,128]{1,0:T(8,128)S(1)} %collective-permute-done.6.west, f32[24,128]{1,0:T(8,128)S(1)} %collective-permute-done.7.east, f32[8,128]{1,0:T(8,128)S(1)} %collective-permute-done.8.south, f32[8,128]{1,0:T(8,128)S(1)} %collective-permute-done.9.north, ...), custom_call_target="tpu_custom_call" | custom-call | tf_op jit(solution)/shard_map/pallas_call | solution.py:400
  (4 shorter events, 0.0 us)
Async XLA Ops:
  0.0 0.9 %copy-start = (f32[512,128]{1,0:T(8,128)S(1)}, f32[512,128]{1,0:T(8,128)}, u32[]{:S(2)}) copy-start(f32[512,128]{1,0:T(8,128)} %get-tuple-element.15.state) | copy-start | bytes 786436 | tf_op jit(solution)/shard_map/cond
  1.0 0.7 %copy-start.2 = (f32[48,128]{1,0:T(8,128)S(1)}, f32[48,128]{1,0:T(8,128)}, u32[]{:S(2)}) copy-start(f32[48,128]{1,0:T(8,128)} %get-tuple-element.16.metric) | copy-start | bytes 73732 | tf_op jit(solution)/shard_map/cond
  1.7 6.1 %collective-permute-start = (f32[280,128]{1,0:T(8,128)S(1)}, f32[280,128]{1,0:T(8,128)S(1)}, u32[]{:S(2)}, u32[]{:S(2)}) collective-permute-start(f32[280,128]{1,0:T(8,128)S(1)} %get-tuple-element.17), channel_id=1, source_target_pairs={{0,8},{1,9},{2,10},{3,11},{4,12},{5,13},{6,14},{7,15},{8,16},{9,17... | collective-permute-start | bytes 430088 | tf_op jit(solution)/shard_map/cond/branch_0_fun/ppermute | solution.py:427
  5.7 5.8 %collective-permute-start.1 = (f32[280,128]{1,0:T(8,128)S(1)}, f32[280,128]{1,0:T(8,128)S(1)}, u32[]{:S(2)}, u32[]{:S(2)}) collective-permute-start(f32[280,128]{1,0:T(8,128)S(1)} %get-tuple-element.18), channel_id=1, source_target_pairs={{8,0},{9,1},{10,2},{11,3},{12,4},{13,5},{14,6},{15,7},{16,8},{17,9... | collective-permute-start | bytes 430088 | tf_op jit(solution)/shard_map/cond/branch_0_fun/ppermute | solution.py:427
  12.0 10.7 %collective-permute-start.4 = (f32[96,128]{1,0:T(8,128)S(1)}, f32[96,128]{1,0:T(8,128)S(1)}, u32[]{:S(2)}, u32[]{:S(2)}) collective-permute-start(f32[96,128]{1,0:T(8,128)S(1)} %get-tuple-element.54), channel_id=1, source_target_pairs={{1,2},{2,1},{3,4},{4,3},{5,6},{6,5},{9,10},{10,9},{11,12},{12,11},... | collective-permute-start | bytes 147464 | tf_op jit(solution)/shard_map/ppermute | solution.py:498
  18.1 5.3 %collective-permute-start.5 = (f32[96,128]{1,0:T(8,128)S(1)}, f32[96,128]{1,0:T(8,128)S(1)}, u32[]{:S(2)}, u32[]{:S(2)}) collective-permute-start(f32[96,128]{1,0:T(8,128)S(1)} %get-tuple-element.55), channel_id=1, source_target_pairs={{0,1},{1,0},{2,3},{3,2},{4,5},{5,4},{6,7},{7,6},{8,9},{9,8},{10,11... | collective-permute-start | bytes 147464 | tf_op jit(solution)/shard_map/ppermute | solution.py:498
  20.0 37.7 %collective-permute-start.6 = (f32[24,128]{1,0:T(8,128)S(1)}, f32[24,128]{1,0:T(8,128)S(1)}, u32[]{:S(2)}, u32[]{:S(2)}) collective-permute-start(f32[24,128]{1,0:T(8,128)S(1)} %get-tuple-element.56), channel_id=1, source_target_pairs={{455,6},{463,4},{471,2},{479,1},{487,0},{495,3},{503,5},{511,7},{4... | collective-permute-start | bytes 36872 | tf_op jit(solution)/shard_map/ppermute | solution.py:484
  21.3 36.4 %collective-permute-start.7 = (f32[24,128]{1,0:T(8,128)S(1)}, f32[24,128]{1,0:T(8,128)S(1)}, u32[]{:S(2)}, u32[]{:S(2)}) collective-permute-start(f32[24,128]{1,0:T(8,128)S(1)} %get-tuple-element.57), channel_id=1, source_target_pairs={{455,62},{463,60},{471,58},{479,57},{487,56},{495,59},{503,61},{51... | collective-permute-start | bytes 36872 | tf_op jit(solution)/shard_map/ppermute | solution.py:484
  22.0 3.4 %collective-permute-start.9 = (f32[8,128]{1,0:T(8,128)S(1)}, f32[8,128]{1,0:T(8,128)S(1)}, u32[]{:S(2)}, u32[]{:S(2)}) collective-permute-start(f32[8,128]{1,0:T(8,128)S(1)} %get-tuple-element.58), channel_id=1, source_target_pairs={{455,7},{463,15},{471,23},{479,31},{487,39},{495,47},{503,55},{511... | collective-permute-start | bytes 12296 | tf_op jit(solution)/shard_map/ppermute | solution.py:484
  22.7 2.7 %collective-permute-start.8 = (f32[8,128]{1,0:T(8,128)S(1)}, f32[8,128]{1,0:T(8,128)S(1)}, u32[]{:S(2)}, u32[]{:S(2)}) collective-permute-start(f32[8,128]{1,0:T(8,128)S(1)} %get-tuple-element.58), channel_id=1, source_target_pairs={{455,0},{463,8},{471,16},{479,24},{487,32},{495,40},{503,48},{511,... | collective-permute-start | bytes 12296 | tf_op jit(solution)/shard_map/ppermute | solution.py:484
  23.4 34.4 %copy-start.4 = (s32[7,4]{0,1:T(4,128)S(1)}, s32[7,4]{0,1:T(4,128)}, u32[]{:S(2)}) copy-start(s32[7,4]{0,1:T(4,128)} %param.9) | copy-start | bytes 340
